TPU v7x, 32 devices: a whole 2x2x4 slice. The times are simulated.
32 devices in a mesh: dp: 8 (over z, x), ctx: 4 (over y, core).
Axes of the slice: x: 2, y: 2, z: 4, core: 2. Of those that a mesh axis runs over, the one named last changes fastest.
Arguments:
- inputs: bfloat16 [8, 512, 2048], P('dp', 'ctx'), may hold values from -8 to 8
- doc_ids: int32 [8, 512], P('dp', 'ctx'), may hold values from 0 to 3, never falling along the last dimension, each value on 1 to 256 neighbouring positions
- dilation: int32 [1], replicated, may hold values from 1 to 256
- filter_w: bfloat16 [2, 2048, 2048], P(None, 'dp', 'ctx'), may hold values from -0.09375 to 0.09375
- gate_w: bfloat16 [2, 2048, 2048], P(None, 'dp', 'ctx'), may hold values from -0.09375 to 0.09375
- filter_m: float32 [2, 2048, 2048], P(None, 'dp', 'ctx'), may hold values from -0.01171875 to 0.01171875
- filter_v: float32 [2, 2048, 2048], P(None, 'dp', 'ctx'), may hold values from 1e-07 to 4e-06
- gate_m: float32 [2, 2048, 2048], P(None, 'dp', 'ctx'), may hold values from -0.01171875 to 0.01171875
- gate_v: float32 [2, 2048, 2048], P(None, 'dp', 'ctx'), may hold values from 1e-07 to 4e-06
- cotangent: bfloat16 [8, 512, 2048], P('dp', 'ctx'), may hold values from -6 to 6
Outputs:
- layer_out: bfloat16 [8, 512, 2048], P('dp', 'ctx')
- input_grad: bfloat16 [8, 512, 2048], P('dp', 'ctx')
- new_filter_w: bfloat16 [2, 2048, 2048], P(None, 'dp', 'ctx')
- new_gate_w: bfloat16 [2, 2048, 2048], P(None, 'dp', 'ctx')
- new_filter_m: float32 [2, 2048, 2048], P(None, 'dp', 'ctx')
- new_filter_v: float32 [2, 2048, 2048], P(None, 'dp', 'ctx')
- new_gate_m: float32 [2, 2048, 2048], P(None, 'dp', 'ctx')
- new_gate_v: float32 [2, 2048, 2048], P(None, 'dp', 'ctx')
Inputs may be any that keep to these rules, and one draw needn't show every extreme that they name: `doc_ids`: document numbers never fall along a sequence; a document covers at most 256 positions.
All inputs are finite; a program needn't handle non-finite values.
Results may differ from a plain program's by a relative error of at most 0.0075.
Values may be sent and summed in bfloat16 or wider, within the bound.
No kernel may reach another device: no remote copies, remote signals or barrier semaphores. Data moves between devices by JAX's collectives and lax.ppermute only.
A program may use at most 128 MiB of HBM per device.

v0:
```python
import jax
import jax.numpy as jnp
from jax import lax
from jax.sharding import PartitionSpec as P

STEP = 10

BETA_ONE = 0.9
BETA_TWO = 0.95
LEARN_RATE = 0.001
EPSILON = 1e-08

AXES = ("dp", "ctx")


def adam_update(weight, moment, second, gradient):
    new_moment = BETA_ONE * moment + (1.0 - BETA_ONE) * gradient
    new_second = BETA_TWO * second + (1.0 - BETA_TWO) * gradient * gradient
    first_fix = 1.0 - BETA_ONE**STEP
    second_fix = 1.0 - BETA_TWO**STEP
    step_size = new_moment / first_fix / (jnp.sqrt(new_second / second_fix) + EPSILON)
    new_weight = (weight.astype(jnp.float32) - LEARN_RATE * step_size).astype(jnp.bfloat16)
    return (new_weight, new_moment, new_second)


def lagged_rows(rows, marks, shift_by):
    length = rows.shape[0]
    padded = jnp.concatenate([jnp.zeros_like(rows), rows], axis=0)
    shifted = lax.dynamic_slice_in_dim(padded, length - shift_by, length, 0)
    mark_padded = jnp.concatenate([jnp.zeros_like(marks), marks], axis=0)
    mark_shifted = lax.dynamic_slice_in_dim(mark_padded, length - shift_by, length, 0)
    return jnp.where(mark_shifted == marks, shifted, jnp.zeros_like(shifted))


def leading_rows(values, marks, shift_by):
    length = values.shape[0]
    padded = jnp.concatenate([values, jnp.zeros_like(values)], axis=0)
    ahead = lax.dynamic_slice_in_dim(padded, shift_by, length, 0)
    mark_padded = jnp.concatenate([marks, jnp.zeros_like(marks)], axis=0)
    mark_ahead = lax.dynamic_slice_in_dim(mark_padded, shift_by, length, 0)
    return jnp.where(mark_ahead == marks, ahead, jnp.zeros_like(ahead))


def activate(own, got, cot):
    wide = cot.shape[1]
    pre = own + got
    filter_tanh = jnp.tanh(pre[:, :wide])
    gate_sigmoid = jax.nn.sigmoid(pre[:, wide:])
    cot = cot.astype(jnp.float32)
    gated = (filter_tanh * gate_sigmoid).astype(jnp.bfloat16)
    filter_delta = cot * gate_sigmoid * (1.0 - filter_tanh * filter_tanh)
    gate_delta = cot * filter_tanh * gate_sigmoid * (1.0 - gate_sigmoid)
    delta = jnp.concatenate([filter_delta, gate_delta], axis=1).astype(jnp.bfloat16)
    return gated, delta


def swapped(i, c):
    return (i & ~2) | ((c & 1) << 1), (c & ~1) | ((i >> 1) & 1)


def make_maps(dp, ctx):
    def line(label):
        return label[0] * ctx + label[1]

    labels = [(i, c) for i in range(dp) for c in range(ctx)]

    def enter(di, dc):
        return [(line(l), line(swapped(l[0] ^ di, l[1] ^ dc))) for l in labels]

    def inner(di, dc):
        return [(line(swapped(*l)), line(swapped(l[0] ^ di, l[1] ^ dc))) for l in labels]

    def leave(di, dc):
        return [(line(swapped(*l)), line((l[0] ^ di, l[1] ^ dc))) for l in labels]

    def plain(di, dc):
        return [(line(l), line((l[0] ^ di, l[1] ^ dc))) for l in labels]

    return enter, inner, leave, plain


def send(value, pairs):
    return lax.ppermute(value, AXES, [(a, b) for a, b in pairs if a != b])


def dot(a, b):
    return jnp.dot(a, b, preferred_element_type=jnp.float32)


def dot_t(a, b):
    return lax.dot_general(a, b, (((1,), (1,)), ((), ())), preferred_element_type=jnp.float32)


def t_dot(a, b):
    return lax.dot_general(a, b, (((0,), (0,)), ((), ())), preferred_element_type=jnp.float32)


def placed_rows(pieces, label):
    size = pieces[0].shape[0]
    whole = jnp.zeros((size * len(pieces),) + pieces[0].shape[1:], pieces[0].dtype)
    for m, piece in enumerate(pieces):
        whole = lax.dynamic_update_slice_in_dim(whole, piece, (label ^ m) * size, 0)
    return whole


def placed_cols(pieces, label):
    stacked = jnp.stack(pieces)
    return jnp.concatenate(
        [
            lax.dynamic_index_in_dim(stacked, label ^ t, 0, keepdims=False)
            for t in range(len(pieces))
        ],
        axis=1,
    )


CHUNKS = 2


def per_device(
    inputs, doc_ids, dilation, filter_w, gate_w, filter_m, filter_v, gate_m, gate_v, cotangent
):
    dp, ctx = lax.axis_size("dp"), lax.axis_size("ctx")
    enter, inner, leave, plain = make_maps(dp, ctx)
    i, c = lax.axis_index("dp"), lax.axis_index("ctx")
    vi, vc = swapped(i, c)
    core = c & 1
    vy = c >> 1
    home = core == ((i >> 1) & 1)
    rows = filter_w.shape[1]
    columns = filter_w.shape[2]
    wide = columns // CHUNKS
    tokens = inputs.shape[1]
    length = tokens * ctx
    shift_by = dilation[0]
    far = list(range(0, dp, 4))
    spans = [j + xx for j in far for xx in (0, 1)]
    others = range(1, ctx // 2)
    bf16, f32 = jnp.bfloat16, jnp.float32

    packed = [
        jnp.concatenate(
            [w[:, :, n * wide : (n + 1) * wide] for w in (filter_w, gate_w)], axis=2
        )
        for n in range(CHUNKS)
    ]
    block = {}

    def kept(own, got):
        return jnp.where(home, own, got)

    def fetch(n, j):
        got = send(packed[n], enter(j, 0))
        block[n, j] = got if j else kept(packed[n], got)

    def relay(n, j):
        block[n, j + 1] = send(block[n, j], inner(1, 0))

    mine = inputs[0]

    def channels(label):
        return jnp.concatenate(
            [lax.dynamic_slice_in_dim(mine, (label ^ o) * rows, rows, 1) for o in spans] + [marks],
            axis=1,
        )

    def pair(own, got):
        low, high = jnp.where(core == 0, own, got), jnp.where(core == 0, got, own)
        return jnp.concatenate([low, high], axis=0)

    for j in far[1:]:
        fetch(0, j)
    fetch(0, 0)
    lanes = 128
    marks = jnp.broadcast_to((doc_ids[0] + 1).astype(bf16)[:, None], (tokens, lanes))
    half = pair(channels(vi), send(channels(vi ^ 2), plain(0, 1)))

    def odd(value):
        return jnp.concatenate(
            [value[:, (2 * n + 1) * rows : (2 * n + 2) * rows] for n in range(len(far))]
            + [value[:, len(spans) * rows :]],
            axis=1,
        )

    def even(value):
        return jnp.concatenate(
            [value[:, 2 * n * rows : (2 * n + 1) * rows] for n in range(len(far))], axis=1
        )

    z_half = send(half, plain(2, 0))
    y_half = [send(half, plain(0, 2 * dy)) for dy in others]
    side_half = send(odd(half), plain(1, 0))
    yz_half = [send(z_half, plain(0, 2 * dy)) for dy in others]
    side_both = jnp.concatenate([side_half, send(odd(z_half), plain(1, 0))], axis=1)
    side_parts = [side_both] + [send(side_both, plain(0, 2 * dy)) for dy in others]
    for j in far[1:]:
        fetch(1, j)
    fetch(1, 0)
    for n in range(CHUNKS):
        for j in far:
            relay(n, j)

    def in_order(here, there):
        return [jnp.where(home, here, there), jnp.where(home, there, here)]

    sequences = in_order(
        placed_rows([half] + y_half, vy), placed_rows([z_half] + yz_half, vy)
    )
    ids_here = [x[:, len(spans) * rows :][:, :1] for x in sequences]
    sequences = [x[:, : len(spans) * rows] for x in sequences]
    side_whole = placed_rows(side_parts, vy)
    width = side_whole.shape[1] // 2
    side = in_order(side_whole[:, :width], side_whole[:, width:])
    ids_side = [x[:, len(far) * rows :][:, :1] for x in side]
    side = [x[:, : len(far) * rows] for x in side]
    lagged = [lagged_rows(x, d, shift_by) for x, d in zip(sequences, ids_here)]
    taps = [[], []]
    for q in (0, 1):
        for n in range(len(spans)):
            cut = slice(n * rows, (n + 1) * rows)
            taps[q].append(jnp.concatenate([sequences[q][:, cut], lagged[q][:, cut]], axis=1))
    group = [
        jnp.concatenate([even(x), even(l)], axis=1) for x, l in zip(sequences, lagged)
    ] + [
        jnp.concatenate([x, lagged_rows(x, ids_side[q], shift_by)], axis=1)
        for q, x in enumerate(side)
    ]

    own_cols = 2 * columns
    cot_parts = [lax.dynamic_slice_in_dim(cotangent[0], vy * own_cols, own_cols, 1)] + [
        send(
            lax.dynamic_slice_in_dim(cotangent[0], (vy ^ dy) * own_cols, own_cols, 1),
            plain(0, 2 * dy),
        )
        for dy in others
    ]
    cot_rows = jnp.stack(cot_parts)
    cot_cuts = [
        lax.dynamic_slice_in_dim(cot_rows, (core ^ e) * columns, columns, 2) for e in (0, 1)
    ]
    cot_got = [send(cot_cuts[e], enter(0, e)) for e in (0, 1)]
    cot_got[0] = kept(cot_cuts[0], cot_got[0])
    cot_cols = placed_rows(
        [cot_got[m & 1][m >> 1] for m in range(ctx)], vc
    )

    gated, delta, grads, backs = [], [], [], []
    for n in range(CHUNKS):
        pre = []
        for q in (1, 0):
            total = None
            for j in far:
                for xx in (0, 1):
                    w = block[n, j + xx].reshape(2 * rows, 2 * wide)
                    term = dot(taps[q][spans.index(j + xx)], w)
                    total = term if total is None else total + term
            pre.append(total)
        got = send(pre[0], inner(2, 0))
        cot = cot_cols[:, n * wide : (n + 1) * wide]
        if n:
            cot, _ = lax.optimization_barrier((cot, delta[-1][0]))
        gated_n, here = activate(pre[1], got, cot)
        gated.append(gated_n)
        across = send(here, inner(1, 0))
        beside = send(here, inner(2, 0))
        diagonal = send(across, inner(2, 0))
        delta.append([here, beside])
        part = []
        for q, d in enumerate(delta[n]):
            if n:
                d, _ = lax.optimization_barrier((d, backs[-1][q][0]))
            ahead = leading_rows(d, ids_here[q], shift_by)
            part.append(
                {
                    o: dot_t(d, block[n, o][0]) + dot_t(ahead, block[n, o][1])
                    for o in spans
                }
            )
        backs.append(part)
        total = None
        for x, d in zip(group, (here, beside, across, diagonal)):
            term = t_dot(x, d)
            total = term if total is None else total + term
        parts = total.astype(bf16).reshape(2, len(far), rows, 2 * wide)
        got = [send(parts[:, m], leave(j, 0)) for m, j in enumerate(far)]
        got[0] = kept(parts[:, 0], got[0])
        grads.append(got)

    gated = jnp.concatenate(gated, axis=1)
    out_cuts = [
        lax.dynamic_slice_in_dim(gated, (vc ^ m) * tokens, tokens, 0) for m in range(ctx)
    ]
    out_pieces = [send(out_cuts[m], leave(0, m)) for m in range(ctx)]
    out_pieces[0] = kept(out_cuts[0], out_pieces[0])
    gated_rows = placed_cols(out_pieces, c)
    layer_out = (mine.astype(f32) + gated_rows.astype(f32)).astype(bf16)

    def half_of(value, label):
        return lax.dynamic_slice_in_dim(value, label * 2 * tokens, 2 * tokens, 0)

    chip_sums = []
    for q in (0, 1):
        back = jnp.concatenate(
            [sum(backs[n][q][o] for n in range(CHUNKS)) for o in spans], axis=1
        )
        kept_rows = half_of(back, vy)
        for dy in others:
            piece = half_of(back, vy ^ dy).astype(bf16)
            kept_rows = kept_rows + send(piece, plain(0, 2 * dy)).astype(f32)
        chip_sums.append(kept_rows)
    chip_sum = in_order(*chip_sums)
    crossing = chip_sum[1].astype(bf16)
    z_got = send(crossing, plain(2, 0)).astype(f32)
    both_sum = (chip_sum[0] + z_got).astype(bf16)
    keep = lax.dynamic_slice_in_dim(both_sum, core * tokens, tokens, 0)
    give = lax.dynamic_slice_in_dim(both_sum, (1 - core) * tokens, tokens, 0)
    got = send(give, plain(0, 1))
    joined = jnp.concatenate([keep, got], axis=1)
    where_is = []
    for t in range(dp):
        rel = vi ^ t
        slot = (rel >> 2) * 2 + (rel & 1) + ((rel >> 1) & 1) * len(spans)
        where_is.append(lax.dynamic_slice_in_dim(joined, slot * rows, rows, 1))
    input_sum = jnp.concatenate(where_is, axis=1).astype(f32)
    input_grad = (cotangent[0].astype(f32) + input_sum).astype(bf16)

    totals = []
    for parts in grads:
        summed = parts[0].astype(f32)
        for part in parts[1:]:
            summed = summed + part.astype(f32)
        totals.append(summed / (length * dp))
    filter_grad = jnp.concatenate([t[:, :, :wide] for t in totals], axis=2)
    gate_grad = jnp.concatenate([t[:, :, wide:] for t in totals], axis=2)
    new_filter_w, new_filter_m, new_filter_v = adam_update(
        filter_w, filter_m, filter_v, filter_grad
    )
    new_gate_w, new_gate_m, new_gate_v = adam_update(gate_w, gate_m, gate_v, gate_grad)
    return (
        layer_out[None],
        input_grad[None],
        new_filter_w,
        new_gate_w,
        new_filter_m,
        new_filter_v,
        new_gate_m,
        new_gate_v,
    )


def solution(mesh):
    seq, par = P("dp", "ctx", None), P(None, "dp", "ctx")

    return jax.shard_map(
        per_device,
        mesh=mesh,
        in_specs=(seq, P("dp", "ctx"), P(), par, par, par, par, par, par, seq),
        out_specs=(seq, seq, par, par, par, par, par, par),
        check_vma=False,
    )
```

profile of v0, /device:TPU:0, one launch (start us, length us, event | category | flops | bytes accessed | tf_op | source)
XLA Modules:
  0.0 250.5 jit_solution(1406303316393797172)
XLA Ops:
  0.7 1.2 constant_dynamic-slice_fusion.18
  7.5 0.8 copy.60
  8.4 3.0 %collective-permute-start.18 = (bf16[128,1024]{0,1:T(8,128)(2,1)}, bf16[128,1024]{0,1:T(8,128)(2,1)}, u32[]{:S(2)}, u32[]{:S(2)}) collective-permute-start(bf16[128,1024]{0,1:T(8,128)(2,1)} %bitcast.22), channel_id=1, source_target_pairs={{0,2},{1,3},{2,0},{3,1},{4,6},{5,7},{6,4},{7,5},{8,10},{9,11},{10,... | collective-permute-start | bytes 786440 | tf_op jit(solution)/shard_map/ppermute | solution.py:83
  11.5 2.7 %collective-permute-start.6 = (bf16[2,256,512]{2,1,0:T(8,128)(2,1)S(1)}, bf16[2,256,512]{2,1,0:T(8,128)(2,1)S(1)}, u32[]{:S(2)}, u32[]{:S(2)}) collective-permute-start(bf16[2,256,512]{2,1,0:T(8,128)(2,1)S(1)} %pad_maximum_fusion.14), channel_id=1, source_target_pairs={{0,16},{1,24},{2,18},{3,26},{4,20},{5,28},{6,22},{7,30},{8,17},{9,... | collective-permute-start | bytes 1572872 | tf_op jit(solution)/shard_map/ppermute | solution.py:83
  14.1 1.5 collective-permute-start.4
  15.6 0.8 pad_maximum_fusion.22
  16.8 1.0 copy.42
  19.5 1.0 fusion.50
  21.2 1.0 broadcast_select_fusion.7
  22.5 31.7 %collective-permute-start.20 = (bf16[2,128,512]{1,2,0:T(8,128)(2,1)S(1)}, bf16[2,128,512]{1,2,0:T(8,128)(2,1)S(1)}, u32[]{:S(2)}, u32[]{:S(2)}) collective-permute-start(bf16[2,128,512]{1,2,0:T(8,128)(2,1)S(1)} %get-tuple-element.88), channel_id=1, source_target_pairs={{0,8},{1,0},{2,10},{3,2},{4,12},{5,4},{6,14},{7,6},{8,9},{9,1},{10... | collective-permute-start | bytes 786440 | tf_op jit(solution)/shard_map/ppermute | solution.py:83
  55.1 1.1 collective-permute-start.2
  56.4 4.6 %collective-permute-done.20 = bf16[2,128,512]{1,2,0:T(8,128)(2,1)S(1)} collective-permute-done((bf16[2,128,512]{1,2,0:T(8,128)(2,1)S(1)}, bf16[2,128,512]{1,2,0:T(8,128)(2,1)S(1)}, u32[]{:S(2)}, u32[]{:S(2)}) %collective-permute-start.20) | collective-permute-done | bytes 262176 | tf_op jit(solution)/shard_map/ppermute | solution.py:83
  61.0 1.5 collective-permute-start.27
  62.6 8.2 %collective-permute-done.27 = bf16[256,640]{0,1:T(8,128)(2,1)S(1)} collective-permute-done((bf16[256,640]{0,1:T(8,128)(2,1)S(1)}, bf16[256,640]{0,1:T(8,128)(2,1)S(1)}, u32[]{:S(2)}, u32[]{:S(2)}) %collective-permute-start.27) | collective-permute-done | bytes 327712 | tf_op jit(solution)/shard_map/ppermute | solution.py:83
  70.8 1.5 collective-permute-start.5
  72.4 1.6 collective-permute-start.28
  74.1 1.1 collective-permute-start.3
  75.8 1.5 collective-permute-start.7
  77.4 15.2 %collective-permute-done.28 = bf16[256,640]{0,1:T(8,128)(2,1)S(1)} collective-permute-done((bf16[256,640]{0,1:T(8,128)(2,1)S(1)}, bf16[256,640]{0,1:T(8,128)(2,1)S(1)}, u32[]{:S(2)}, u32[]{:S(2)}) %collective-permute-start.28) | collective-permute-done | bytes 327712 | tf_op jit(solution)/shard_map/ppermute | solution.py:83
  92.6 1.5 collective-permute-start.12
  95.0 1.1 fusion.16
  97.9 17.2 %collective-permute-done.7 = bf16[2,256,512]{2,1,0:T(8,128)(2,1)S(1)} collective-permute-done((bf16[2,256,512]{2,1,0:T(8,128)(2,1)S(1)}, bf16[2,256,512]{2,1,0:T(8,128)(2,1)S(1)}, u32[]{:S(2)}, u32[]{:S(2)}) %collective-permute-start.7) | collective-permute-done | bytes 524320 | tf_op jit(solution)/shard_map/ppermute | solution.py:83
  119.3 5.4 %collective-permute-done.12 = bf16[2,256,512]{2,1,0:T(8,128)(2,1)S(1)} collective-permute-done((bf16[2,256,512]{2,1,0:T(8,128)(2,1)S(1)}, bf16[2,256,512]{2,1,0:T(8,128)(2,1)S(1)}, u32[]{:S(2)}, u32[]{:S(2)}) %collective-permute-start.12) | collective-permute-done | bytes 524320 | tf_op jit(solution)/shard_map/ppermute | solution.py:83
  126.8 1.5 fusion.34
  131.7 2.1 fusion.71
  133.7 2.0 fusion.72
  136.0 1.6 collective-permute-start.16
  138.3 1.4 fusion.52
  140.0 2.7 %collective-permute-start.23 = (bf16[512,512]{0,1:T(8,128)(2,1)S(1)}, bf16[512,512]{0,1:T(8,128)(2,1)}, u32[]{:S(2)}, u32[]{:S(2)}) collective-permute-start(bf16[512,512]{0,1:T(8,128)(2,1)S(1)} %pad_maximum_fusion.25), channel_id=1, source_target_pairs={{0,1},{8,9},{2,3},{10,11},{4,5},{12,13},{6,7},{14,15},{1,0},{9,8},... | collective-permute-start | bytes 1572872 | tf_op jit(solution)/shard_map/ppermute | solution.py:83
  143.9 1.4 fusion.65
  145.8 1.4 fusion.60
  147.7 1.4 fusion.56
  151.3 0.9 dynamic-slice_convert_fusion.1
  152.2 1.6 collective-permute-start.34
  154.3 2.8 %collective-permute-done.15 = bf16[128,512]{0,1:T(8,128)(2,1)S(1)} collective-permute-done((bf16[128,512]{0,1:T(8,128)(2,1)S(1)}, bf16[128,512]{0,1:T(8,128)(2,1)S(1)}, u32[]{:S(2)}, u32[]{:S(2)}) %collective-permute-start.15) | collective-permute-done | bytes 131104 | tf_op jit(solution)/shard_map/ppermute | solution.py:83
  157.8 0.9 add_convert_fusion.4
  158.7 2.0 copy.73
  160.8 1.4 fusion.53
  162.2 1.2 convolution_add_fusion.15
  163.5 1.5 fusion.55
  165.0 1.4 fusion.9
  166.8 1.5 fusion.67
  168.3 1.5 fusion.63
  170.3 1.4 fusion.59
  172.6 1.3 convolution_add_fusion.10
  173.9 1.3 convolution_add_fusion.12
  175.3 1.3 fusion.6
  177.6 1.5 collective-permute-start.24
  179.1 1.8 fusion.69
  180.9 1.8 fusion.18
  183.3 1.8 fusion.19
  185.9 3.9 %collective-permute-done.24 = bf16[256,1024]{0,1:T(8,128)(2,1)S(1)} collective-permute-done((bf16[256,1024]{0,1:T(8,128)(2,1)S(1)}, bf16[256,1024]{0,1:T(8,128)(2,1)S(1)}, u32[]{:S(2)}, u32[]{:S(2)}) %collective-permute-start.24) | collective-permute-done | bytes 524320 | tf_op jit(solution)/shard_map/ppermute | solution.py:83
  189.7 1.4 select_convert_fusion
  191.2 2.0 collective-permute-start.25
  196.4 2.3 collective-permute-start.33
  198.7 0.9 collective-permute-start.32
  199.6 11.1 %collective-permute-done.25 = bf16[256,1024]{0,1:T(8,128)(2,1)S(1)} collective-permute-done((bf16[256,1024]{0,1:T(8,128)(2,1)S(1)}, bf16[256,1024]{0,1:T(8,128)(2,1)S(1)}, u32[]{:S(2)}, u32[]{:S(2)}) %collective-permute-start.25) | collective-permute-done | bytes 524320 | tf_op jit(solution)/shard_map/ppermute | solution.py:83
  210.7 1.4 add_convert_fusion.3
  212.3 20.0 %collective-permute-done.37 = bf16[2,256,512]{2,1,0:T(8,128)(2,1)S(1)} collective-permute-done((bf16[2,256,512]{2,1,0:T(8,128)(2,1)S(1)}, bf16[2,256,512]{2,1,0:T(8,128)(2,1)S(1)}, u32[]{:S(2)}, u32[]{:S(2)}) %collective-permute-start.37) | collective-permute-done | bytes 524320 | tf_op jit(solution)/shard_map/ppermute | solution.py:83
  232.7 8.9 %collective-permute-done.33 = bf16[2,256,512]{2,1,0:T(8,128)(2,1)S(1)} collective-permute-done((bf16[2,256,512]{2,1,0:T(8,128)(2,1)S(1)}, bf16[2,256,512]{2,1,0:T(8,128)(2,1)S(1)}, u32[]{:S(2)}, u32[]{:S(2)}) %collective-permute-start.33) | collective-permute-done | bytes 524320 | tf_op jit(solution)/shard_map/ppermute | solution.py:83
  242.0 2.0 subtract_convert_fusion.1
  244.5 2.0 subtract_convert_fusion
  246.6 1.4 fusion.82
  249.6 0.9 add_convert_fusion.2
  (276 shorter events, 37.6 us)
Async XLA Ops:
  0.6 6.9 %copy-start.31 = (bf16[1,128,2048]{2,1,0:T(8,128)(2,1)S(1)}, bf16[1,128,2048]{2,1,0:T(8,128)(2,1)}, u32[]{:S(2)}) copy-start(bf16[1,128,2048]{2,1,0:T(8,128)(2,1)} %param.19) | copy-start | bytes 1572868
  1.9 9.5 %copy-start.35 = (bf16[2,256,512]{2,1,0:T(8,128)(2,1)S(1)}, bf16[2,256,512]{2,1,0:T(8,128)(2,1)}, u32[]{:S(2)}) copy-start(bf16[2,256,512]{2,1,0:T(8,128)(2,1)} %param.13) | copy-start | bytes 1572868
  1.9 9.5 %copy-start.37 = (bf16[2,256,512]{2,1,0:T(8,128)(2,1)S(1)}, bf16[2,256,512]{2,1,0:T(8,128)(2,1)}, u32[]{:S(2)}) copy-start(bf16[2,256,512]{2,1,0:T(8,128)(2,1)} %param.14) | copy-start | bytes 1572868
  6.8 13.7 %collective-permute-start = (bf16[128,1152]{0,1:T(8,128)(2,1)}, bf16[128,1152]{0,1:T(8,128)(2,1)}, u32[]{:S(2)}, u32[]{:S(2)}) collective-permute-start(bf16[128,1152]{0,1:T(8,128)(2,1)} %get-tuple-element.113), channel_id=1, source_target_pairs={{0,1},{1,0},{2,3},{3,2},{4,5},{5,4},{6,7},{7,6},{8,9},{9,8},{10,11... | collective-permute-start | bytes 884744 | tf_op jit(solution)/shard_map/ppermute | solution.py:83
  8.4 8.4 %copy-start.34 = (bf16[1,128,2048]{2,1,0:T(8,128)(2,1)S(1)}, bf16[1,128,2048]{2,1,0:T(8,128)(2,1)}, u32[]{:S(2)}) copy-start(bf16[1,128,2048]{2,1,0:T(8,128)(2,1)} %param.10) | copy-start | bytes 1572868
  8.4 10.4 %collective-permute-start.18 = (bf16[128,1024]{0,1:T(8,128)(2,1)}, bf16[128,1024]{0,1:T(8,128)(2,1)}, u32[]{:S(2)}, u32[]{:S(2)}) collective-permute-start(bf16[128,1024]{0,1:T(8,128)(2,1)} %bitcast.22), channel_id=1, source_target_pairs={{0,2},{1,3},{2,0},{3,1},{4,6},{5,7},{6,4},{7,5},{8,10},{9,11},{10,... | collective-permute-start | bytes 786440 | tf_op jit(solution)/shard_map/ppermute | solution.py:83
  11.5 63.8 %collective-permute-start.6 = (bf16[2,256,512]{2,1,0:T(8,128)(2,1)S(1)}, bf16[2,256,512]{2,1,0:T(8,128)(2,1)S(1)}, u32[]{:S(2)}, u32[]{:S(2)}) collective-permute-start(bf16[2,256,512]{2,1,0:T(8,128)(2,1)S(1)} %pad_maximum_fusion.14), channel_id=1, source_target_pairs={{0,16},{1,24},{2,18},{3,26},{4,20},{5,28},{6,22},{7,30},{8,17},{9,... | collective-permute-start | bytes 1572872 | tf_op jit(solution)/shard_map/ppermute | solution.py:83
  14.1 40.2 %collective-permute-start.4 = (bf16[2,256,512]{2,1,0:T(8,128)(2,1)S(1)}, bf16[2,256,512]{2,1,0:T(8,128)(2,1)}, u32[]{:S(2)}, u32[]{:S(2)}) collective-permute-start(bf16[2,256,512]{2,1,0:T(8,128)(2,1)S(1)} %pad_maximum_fusion.14), channel_id=1, source_target_pairs={{1,8},{3,10},{5,12},{7,14},{8,1},{10,3},{12,5},{14,7},{17,24},{19,... | collective-permute-start | bytes 1572872 | tf_op jit(solution)/shard_map/ppermute | solution.py:83
  16.4 59.4 %collective-permute-start.11 = (bf16[2,256,512]{2,1,0:T(8,128)(2,1)}, bf16[2,256,512]{2,1,0:T(8,128)(2,1)S(1)}, u32[]{:S(2)}, u32[]{:S(2)}) collective-permute-start(bf16[2,256,512]{2,1,0:T(8,128)(2,1)} %pad_maximum_fusion.22), channel_id=1, source_target_pairs={{0,16},{1,24},{2,18},{3,26},{4,20},{5,28},{6,22},{7,30},{8,17},{9,... | collective-permute-start | bytes 1572872 | tf_op jit(solution)/shard_map/ppermute | solution.py:83
  17.8 3.4 %copy-start.44 = (bf16[128,1152]{0,1:T(8,128)(2,1)S(1)}, bf16[128,1152]{0,1:T(8,128)(2,1)}, u32[]{:S(2)}) copy-start(bf16[128,1152]{0,1:T(8,128)(2,1)} %copy-done.43) | copy-start | bytes 884740
  18.8 36.3 %collective-permute-start.9 = (bf16[2,256,512]{2,1,0:T(8,128)(2,1)}, bf16[2,256,512]{2,1,0:T(8,128)(2,1)S(1)}, u32[]{:S(2)}, u32[]{:S(2)}) collective-permute-start(bf16[2,256,512]{2,1,0:T(8,128)(2,1)} %pad_maximum_fusion.22), channel_id=1, source_target_pairs={{1,8},{3,10},{5,12},{7,14},{8,1},{10,3},{12,5},{14,7},{17,24},{19,... | collective-permute-start | bytes 1572872 | tf_op jit(solution)/shard_map/ppermute | solution.py:83
  20.5 2.0 collective-permute-start.19
  22.5 38.4 %collective-permute-start.20 = (bf16[2,128,512]{1,2,0:T(8,128)(2,1)S(1)}, bf16[2,128,512]{1,2,0:T(8,128)(2,1)S(1)}, u32[]{:S(2)}, u32[]{:S(2)}) collective-permute-start(bf16[2,128,512]{1,2,0:T(8,128)(2,1)S(1)} %get-tuple-element.88), channel_id=1, source_target_pairs={{0,8},{1,0},{2,10},{3,2},{4,12},{5,4},{6,14},{7,6},{8,9},{9,1},{10... | collective-permute-start | bytes 786440 | tf_op jit(solution)/shard_map/ppermute | solution.py:83
  54.3 19.8 %collective-permute-start.1 = (bf16[256,1152]{0,1:T(8,128)(2,1)S(1)}, bf16[256,1152]{0,1:T(8,128)(2,1)S(1)}, u32[]{:S(2)}, u32[]{:S(2)}) collective-permute-start(bf16[256,1152]{0,1:T(8,128)(2,1)S(1)} %get-tuple-element.75), channel_id=1, source_target_pairs={{0,2},{1,3},{2,0},{3,1},{4,6},{5,7},{6,4},{7,5},{8,10},{9,11},{10,... | collective-permute-start | bytes 1769480 | tf_op jit(solution)/shard_map/ppermute | solution.py:83
  55.0 84.7 %copy-start.4 = (bf16[2,256,512]{2,1,0:T(8,128)(2,1)}, bf16[2,256,512]{2,1,0:T(8,128)(2,1)S(1)}, u32[]{:S(2)}) copy-start(bf16[2,256,512]{2,1,0:T(8,128)(2,1)S(1)} %broadcast_select_fusion.5) | copy-start | bytes 1572868
  55.1 17.2 %collective-permute-start.2 = (bf16[256,1152]{0,1:T(8,128)(2,1)S(1)}, bf16[256,1152]{0,1:T(8,128)(2,1)S(1)}, u32[]{:S(2)}, u32[]{:S(2)}) collective-permute-start(bf16[256,1152]{0,1:T(8,128)(2,1)S(1)} %get-tuple-element.75), channel_id=1, source_target_pairs={{0,8},{1,9},{2,10},{3,11},{4,12},{5,13},{6,14},{7,15},{8,0},{9,1},... | collective-permute-start | bytes 1769480 | tf_op jit(solution)/shard_map/ppermute | solution.py:83
  56.4 86.8 %copy-start.5 = (bf16[2,256,512]{2,1,0:T(8,128)(2,1)}, bf16[2,256,512]{2,1,0:T(8,128)(2,1)S(1)}, u32[]{:S(2)}) copy-start(bf16[2,256,512]{2,1,0:T(8,128)(2,1)S(1)} %broadcast_select_fusion.4) | copy-start | bytes 1572868
  61.0 9.8 %collective-permute-start.27 = (bf16[256,640]{0,1:T(8,128)(2,1)S(1)}, bf16[256,640]{0,1:T(8,128)(2,1)S(1)}, u32[]{:S(2)}, u32[]{:S(2)}) collective-permute-start(bf16[256,640]{0,1:T(8,128)(2,1)S(1)} %pad_maximum_fusion.42), channel_id=1, source_target_pairs={{0,4},{1,5},{2,6},{3,7},{4,0},{5,1},{6,2},{7,3},{8,12},{9,13},{10,... | collective-permute-start | bytes 983048 | tf_op jit(solution)/shard_map/ppermute | solution.py:83
  70.8 26.0 %collective-permute-start.5 = (bf16[2,256,512]{2,1,0:T(8,128)(2,1)S(1)}, bf16[2,256,512]{2,1,0:T(8,128)(2,1)S(1)}, u32[]{:S(2)}, u32[]{:S(2)}) collective-permute-start(bf16[2,256,512]{2,1,0:T(8,128)(2,1)S(1)} %broadcast_select_fusion.5), channel_id=1, source_target_pairs={{0,4},{8,12},{2,6},{10,14},{4,0},{12,8},{6,2},{14,10},{1,5},{9,13}... | collective-permute-start | bytes 1572872 | tf_op jit(solution)/shard_map/ppermute | solution.py:83
  72.4 20.2 %collective-permute-start.28 = (bf16[256,640]{0,1:T(8,128)(2,1)S(1)}, bf16[256,640]{0,1:T(8,128)(2,1)S(1)}, u32[]{:S(2)}, u32[]{:S(2)}) collective-permute-start(bf16[256,640]{0,1:T(8,128)(2,1)S(1)} %pad_maximum_fusion.43), channel_id=1, source_target_pairs={{0,4},{1,5},{2,6},{3,7},{4,0},{5,1},{6,2},{7,3},{8,12},{9,13},{10,... | collective-permute-start | bytes 983048 | tf_op jit(solution)/shard_map/ppermute | solution.py:83
  74.1 20.2 %collective-permute-start.3 = (bf16[256,1152]{0,1:T(8,128)(2,1)S(1)}, bf16[256,1152]{0,1:T(8,128)(2,1)S(1)}, u32[]{:S(2)}, u32[]{:S(2)}) collective-permute-start(bf16[256,1152]{0,1:T(8,128)(2,1)S(1)} %collective-permute-done.2), channel_id=1, source_target_pairs={{0,2},{1,3},{2,0},{3,1},{4,6},{5,7},{6,4},{7,5},{8,10},{9,11},{10,... | collective-permute-start | bytes 1769480 | tf_op jit(solution)/shard_map/ppermute | solution.py:83
  75.3 41.0 %copy-start.11 = (bf16[2,256,512]{2,1,0:T(8,128)(2,1)}, bf16[2,256,512]{2,1,0:T(8,128)(2,1)S(1)}, u32[]{:S(2)}) copy-start(bf16[2,256,512]{2,1,0:T(8,128)(2,1)S(1)} %collective-permute-done.6) | copy-start | bytes 1572868
  75.3 42.0 %collective-permute-start.10 = (bf16[2,256,512]{2,1,0:T(8,128)(2,1)S(1)}, bf16[2,256,512]{2,1,0:T(8,128)(2,1)S(1)}, u32[]{:S(2)}, u32[]{:S(2)}) collective-permute-start(bf16[2,256,512]{2,1,0:T(8,128)(2,1)S(1)} %broadcast_select_fusion.4), channel_id=1, source_target_pairs={{0,4},{8,12},{2,6},{10,14},{4,0},{12,8},{6,2},{14,10},{1,5},{9,13}... | collective-permute-start | bytes 1572872 | tf_op jit(solution)/shard_map/ppermute | solution.py:83
  75.8 40.9 %copy-start.14 = (bf16[2,256,512]{2,1,0:T(8,128)(2,1)}, bf16[2,256,512]{2,1,0:T(8,128)(2,1)S(1)}, u32[]{:S(2)}) copy-start(bf16[2,256,512]{2,1,0:T(8,128)(2,1)S(1)} %collective-permute-done.11) | copy-start | bytes 1572868
  75.8 39.2 %collective-permute-start.7 = (bf16[2,256,512]{2,1,0:T(8,128)(2,1)S(1)}, bf16[2,256,512]{2,1,0:T(8,128)(2,1)S(1)}, u32[]{:S(2)}, u32[]{:S(2)}) collective-permute-start(bf16[2,256,512]{2,1,0:T(8,128)(2,1)S(1)} %collective-permute-done.6), channel_id=1, source_target_pairs={{0,4},{8,12},{2,6},{10,14},{4,0},{12,8},{6,2},{14,10},{1,5},{9,13}... | collective-permute-start | bytes 1572872 | tf_op jit(solution)/shard_map/ppermute | solution.py:83
  92.6 32.1 %collective-permute-start.12 = (bf16[2,256,512]{2,1,0:T(8,128)(2,1)S(1)}, bf16[2,256,512]{2,1,0:T(8,128)(2,1)S(1)}, u32[]{:S(2)}, u32[]{:S(2)}) collective-permute-start(bf16[2,256,512]{2,1,0:T(8,128)(2,1)S(1)} %collective-permute-done.11), channel_id=1, source_target_pairs={{0,4},{8,12},{2,6},{10,14},{4,0},{12,8},{6,2},{14,10},{1,5},{9,13}... | collective-permute-start | bytes 1572872 | tf_op jit(solution)/shard_map/ppermute | solution.py:83
  94.3 32.0 %collective-permute-start.29 = (bf16[256,1280]{0,1:T(8,128)(2,1)S(1)}, bf16[256,1280]{0,1:T(8,128)(2,1)S(1)}, u32[]{:S(2)}, u32[]{:S(2)}) collective-permute-start(bf16[256,1280]{0,1:T(8,128)(2,1)S(1)} %constant_dynamic-update-slice_fusion.2), channel_id=1, source_target_pairs={{0,2},{1,3},{2,0},{3,1},{4,6},{5,7},{6,4},{7,5},{8,10},{9,11},{10,... | collective-permute-start | bytes 1966088 | tf_op jit(solution)/shard_map/ppermute | solution.py:83
  96.2 19.6 %copy-start.25 = (bf16[512,256]{0,1:T(8,128)(2,1)}, bf16[512,256]{0,1:T(8,128)(2,1)S(1)}, u32[]{:S(2)}) copy-start(bf16[512,256]{0,1:T(8,128)(2,1)S(1)} %get-tuple-element.53) | copy-start | bytes 786436
  96.3 19.5 %copy-start.27 = (bf16[512,256]{0,1:T(8,128)(2,1)}, bf16[512,256]{0,1:T(8,128)(2,1)S(1)}, u32[]{:S(2)}) copy-start(bf16[512,256]{0,1:T(8,128)(2,1)S(1)} %get-tuple-element.71) | copy-start | bytes 786436
  96.3 22.5 %copy-start.23 = (bf16[512,256]{0,1:T(8,128)(2,1)}, bf16[512,256]{0,1:T(8,128)(2,1)S(1)}, u32[]{:S(2)}) copy-start(bf16[512,256]{0,1:T(8,128)(2,1)S(1)} %get-tuple-element.73) | copy-start | bytes 786436
  96.8 54.0 %copy-start.17 = (bf16[2,256,512]{2,1,0:T(8,128)(2,1)}, bf16[2,256,512]{2,1,0:T(8,128)(2,1)S(1)}, u32[]{:S(2)}) copy-start(bf16[2,256,512]{2,1,0:T(8,128)(2,1)S(1)} %collective-permute-done.5) | copy-start | bytes 1572868
  115.1 35.0 %copy-start.7 = (bf16[2,256,512]{2,1,0:T(8,128)(2,1)}, bf16[2,256,512]{2,1,0:T(8,128)(2,1)S(1)}, u32[]{:S(2)}) copy-start(bf16[2,256,512]{2,1,0:T(8,128)(2,1)S(1)} %collective-permute-done.7) | copy-start | bytes 1572868
  115.6 12.8 %collective-permute-start.8 = (f32[512,512]{0,1:T(8,128)S(1)}, f32[512,512]{0,1:T(8,128)S(1)}, u32[]{:S(2)}, u32[]{:S(2)}) collective-permute-start(f32[512,512]{0,1:T(8,128)S(1)} %convolution_add_fusion.4), channel_id=1, source_target_pairs={{0,1},{8,9},{2,3},{10,11},{4,5},{12,13},{6,7},{14,15},{1,0},{9,8},... | collective-permute-start | bytes 3145736 | tf_op jit(solution)/shard_map/ppermute | solution.py:83
  117.3 32.5 %copy-start.19 = (bf16[2,256,512]{2,1,0:T(8,128)(2,1)}, bf16[2,256,512]{2,1,0:T(8,128)(2,1)S(1)}, u32[]{:S(2)}) copy-start(bf16[2,256,512]{2,1,0:T(8,128)(2,1)S(1)} %collective-permute-done.10) | copy-start | bytes 1572868
  124.7 24.5 %copy-start.21 = (bf16[2,256,512]{2,1,0:T(8,128)(2,1)}, bf16[2,256,512]{2,1,0:T(8,128)(2,1)S(1)}, u32[]{:S(2)}) copy-start(bf16[2,256,512]{2,1,0:T(8,128)(2,1)S(1)} %collective-permute-done.12) | copy-start | bytes 1572868
  125.2 5.4 %collective-permute-start.13 = (f32[512,512]{0,1:T(8,128)S(1)}, f32[512,512]{0,1:T(8,128)S(1)}, u32[]{:S(2)}, u32[]{:S(2)}) collective-permute-start(f32[512,512]{0,1:T(8,128)S(1)} %convolution_add_fusion), channel_id=1, source_target_pairs={{0,1},{8,9},{2,3},{10,11},{4,5},{12,13},{6,7},{14,15},{1,0},{9,8},... | collective-permute-start | bytes 3145736 | tf_op jit(solution)/shard_map/ppermute | solution.py:83
  130.1 30.7 %collective-permute-start.22 = (bf16[512,512]{0,1:T(8,128)(2,1)}, bf16[512,512]{0,1:T(8,128)(2,1)S(1)}, u32[]{:S(2)}, u32[]{:S(2)}) collective-permute-start(bf16[512,512]{0,1:T(8,128)(2,1)} %pad_maximum_fusion.24), channel_id=1, source_target_pairs={{0,1},{8,9},{2,3},{10,11},{4,5},{12,13},{6,7},{14,15},{1,0},{9,8},... | collective-permute-start | bytes 1572872 | tf_op jit(solution)/shard_map/ppermute | solution.py:83
  135.9 16.3 %collective-permute-start.17 = (bf16[128,512]{0,1:T(8,128)(2,1)S(1)}, bf16[128,512]{0,1:T(8,128)(2,1)S(1)}, u32[]{:S(2)}, u32[]{:S(2)}) collective-permute-start(bf16[128,512]{0,1:T(8,128)(2,1)S(1)} %get-tuple-element.99), channel_id=1, source_target_pairs={{0,3},{8,2},{2,1},{10,0},{4,7},{12,6},{6,5},{14,4},{1,11},{9,10},{... | collective-permute-start | bytes 393224 | tf_op jit(solution)/shard_map/ppermute | solution.py:83
  136.0 17.8 %collective-permute-start.16 = (bf16[128,512]{0,1:T(8,128)(2,1)S(1)}, bf16[128,512]{0,1:T(8,128)(2,1)S(1)}, u32[]{:S(2)}, u32[]{:S(2)}) collective-permute-start(bf16[128,512]{0,1:T(8,128)(2,1)S(1)} %get-tuple-element.98), channel_id=1, source_target_pairs={{0,2},{8,3},{2,0},{10,1},{4,6},{12,7},{6,4},{14,5},{1,10},{9,11},{... | collective-permute-start | bytes 393224 | tf_op jit(solution)/shard_map/ppermute | solution.py:83
  137.6 14.5 %collective-permute-start.14 = (bf16[128,512]{0,1:T(8,128)(2,1)S(1)}, bf16[128,512]{0,1:T(8,128)(2,1)S(1)}, u32[]{:S(2)}, u32[]{:S(2)}) collective-permute-start(bf16[128,512]{0,1:T(8,128)(2,1)S(1)} %get-tuple-element.96), channel_id=1, source_target_pairs={{8,1},{10,3},{12,5},{14,7},{1,8},{3,10},{5,12},{7,14},{24,17},{26,... | collective-permute-start | bytes 393224 | tf_op jit(solution)/shard_map/ppermute | solution.py:83
  140.0 23.5 %collective-permute-start.23 = (bf16[512,512]{0,1:T(8,128)(2,1)S(1)}, bf16[512,512]{0,1:T(8,128)(2,1)}, u32[]{:S(2)}, u32[]{:S(2)}) collective-permute-start(bf16[512,512]{0,1:T(8,128)(2,1)S(1)} %pad_maximum_fusion.25), channel_id=1, source_target_pairs={{0,1},{8,9},{2,3},{10,11},{4,5},{12,13},{6,7},{14,15},{1,0},{9,8},... | collective-permute-start | bytes 1572872 | tf_op jit(solution)/shard_map/ppermute | solution.py:83
  151.2 6.5 %copy-start.33 = (bf16[1,128,2048]{1,2,0:T(8,128)(2,1)S(1)}, bf16[1,128,2048]{1,2,0:T(8,128)(2,1)}, u32[]{:S(2)}) copy-start(bf16[1,128,2048]{1,2,0:T(8,128)(2,1)} %copy.42) | copy-start | bytes 1572868
  152.1 5.0 %collective-permute-start.15 = (bf16[128,512]{0,1:T(8,128)(2,1)S(1)}, bf16[128,512]{0,1:T(8,128)(2,1)S(1)}, u32[]{:S(2)}, u32[]{:S(2)}) collective-permute-start(bf16[128,512]{0,1:T(8,128)(2,1)S(1)} %get-tuple-element.97), channel_id=1, source_target_pairs={{0,1},{8,0},{2,3},{10,2},{4,5},{12,4},{6,7},{14,6},{1,9},{9,8},{3,... | collective-permute-start | bytes 393224 | tf_op jit(solution)/shard_map/ppermute | solution.py:83
  152.2 26.9 %collective-permute-start.34 = (bf16[512,512]{0,1:T(8,128)(2,1)S(1)}, bf16[512,512]{0,1:T(8,128)(2,1)}, u32[]{:S(2)}, u32[]{:S(2)}) collective-permute-start(bf16[512,512]{0,1:T(8,128)(2,1)S(1)} %pad_maximum_fusion.25), channel_id=1, source_target_pairs={{0,4},{8,12},{2,6},{10,14},{4,0},{12,8},{6,2},{14,10},{1,5},{9,13}... | collective-permute-start | bytes 1572872 | tf_op jit(solution)/shard_map/ppermute | solution.py:83
  153.8 29.0 %collective-permute-start.30 = (bf16[512,512]{0,1:T(8,128)(2,1)}, bf16[512,512]{0,1:T(8,128)(2,1)}, u32[]{:S(2)}, u32[]{:S(2)}) collective-permute-start(bf16[512,512]{0,1:T(8,128)(2,1)} %pad_maximum_fusion.24), channel_id=1, source_target_pairs={{0,4},{8,12},{2,6},{10,14},{4,0},{12,8},{6,2},{14,10},{1,5},{9,13}... | collective-permute-start | bytes 1572872 | tf_op jit(solution)/shard_map/ppermute | solution.py:83
  157.1 28.7 %collective-permute-start.21 = (bf16[256,1024]{0,1:T(8,128)(2,1)}, bf16[256,1024]{0,1:T(8,128)(2,1)}, u32[]{:S(2)}, u32[]{:S(2)}) collective-permute-start(bf16[256,1024]{0,1:T(8,128)(2,1)} %dynamic-slice_convert_fusion.1), channel_id=1, source_target_pairs={{0,2},{1,3},{2,0},{3,1},{4,6},{5,7},{6,4},{7,5},{8,10},{9,11},{10,... | collective-permute-start | bytes 1572872 | tf_op jit(solution)/shard_map/ppermute | solution.py:83
  166.8 3.5 %copy-start.20 = (bf16[2,256,512]{2,1,0:T(8,128)(2,1)S(1)}, bf16[2,256,512]{2,1,0:T(8,128)(2,1)}, u32[]{:S(2)}) copy-start(bf16[2,256,512]{2,1,0:T(8,128)(2,1)} %copy-done.19) | copy-start | bytes 1572868
  168.3 3.4 %copy-start.18 = (bf16[2,256,512]{2,1,0:T(8,128)(2,1)S(1)}, bf16[2,256,512]{2,1,0:T(8,128)(2,1)}, u32[]{:S(2)}) copy-start(bf16[2,256,512]{2,1,0:T(8,128)(2,1)} %copy-done.17) | copy-start | bytes 1572868
  177.6 3.4 %copy-start.3 = (bf16[512,512]{0,1:T(8,128)(2,1)S(1)}, bf16[512,512]{0,1:T(8,128)(2,1)}, u32[]{:S(2)}) copy-start(bf16[512,512]{0,1:T(8,128)(2,1)} %copy-done.2) | copy-start | bytes 1572868
  177.6 12.2 %collective-permute-start.24 = (bf16[256,1024]{0,1:T(8,128)(2,1)S(1)}, bf16[256,1024]{0,1:T(8,128)(2,1)S(1)}, u32[]{:S(2)}, u32[]{:S(2)}) collective-permute-start(bf16[256,1024]{0,1:T(8,128)(2,1)S(1)} %dynamic-slice_convert_fusion), channel_id=1, source_target_pairs={{0,2},{1,3},{2,0},{3,1},{4,6},{5,7},{6,4},{7,5},{8,10},{9,11},{10,... | collective-permute-start | bytes 1572872 | tf_op jit(solution)/shard_map/ppermute | solution.py:83
  179.1 14.1 %collective-permute-start.35 = (bf16[512,512]{0,1:T(8,128)(2,1)}, bf16[512,512]{0,1:T(8,128)(2,1)S(1)}, u32[]{:S(2)}, u32[]{:S(2)}) collective-permute-start(bf16[512,512]{0,1:T(8,128)(2,1)} %collective-permute-done.34), channel_id=1, source_target_pairs={{0,1},{8,9},{2,3},{10,11},{4,5},{12,13},{6,7},{14,15},{1,0},{9,8},... | collective-permute-start | bytes 1572872 | tf_op jit(solution)/shard_map/ppermute | solution.py:83
  182.7 12.3 %collective-permute-start.31 = (bf16[512,512]{0,1:T(8,128)(2,1)}, bf16[512,512]{0,1:T(8,128)(2,1)S(1)}, u32[]{:S(2)}, u32[]{:S(2)}) collective-permute-start(bf16[512,512]{0,1:T(8,128)(2,1)} %collective-permute-done.30), channel_id=1, source_target_pairs={{0,1},{8,9},{2,3},{10,11},{4,5},{12,13},{6,7},{14,15},{1,0},{9,8},... | collective-permute-start | bytes 1572872 | tf_op jit(solution)/shard_map/ppermute | solution.py:83
  185.8 7.4 %copy-start.1 = (bf16[512,512]{0,1:T(8,128)(2,1)S(1)}, bf16[512,512]{0,1:T(8,128)(2,1)}, u32[]{:S(2)}) copy-start(bf16[512,512]{0,1:T(8,128)(2,1)} %copy-done) | copy-start | bytes 1572868
  185.8 7.4 %copy-start.9 = (bf16[512,512]{0,1:T(8,128)(2,1)S(1)}, bf16[512,512]{0,1:T(8,128)(2,1)}, u32[]{:S(2)}) copy-start(bf16[512,512]{0,1:T(8,128)(2,1)} %get-tuple-element.119) | copy-start | bytes 1572868
  185.8 7.4 %copy-start.30 = (f32[1024,512]{1,0:T(8,128)S(1)}, f32[1024,512]{1,0:T(8,128)}, u32[]{:S(2)}) copy-start(f32[1024,512]{1,0:T(8,128)} %fusion.71) | copy-start | bytes 6291460
  191.2 19.6 %collective-permute-start.25 = (bf16[256,1024]{0,1:T(8,128)(2,1)S(1)}, bf16[256,1024]{0,1:T(8,128)(2,1)S(1)}, u32[]{:S(2)}, u32[]{:S(2)}) collective-permute-start(bf16[256,1024]{0,1:T(8,128)(2,1)S(1)} %select_convert_fusion), channel_id=1, source_target_pairs={{0,8},{1,9},{2,10},{3,11},{4,12},{5,13},{6,14},{7,15},{8,0},{9,1},... | collective-permute-start | bytes 1572872 | tf_op jit(solution)/shard_map/ppermute | solution.py:83
  194.1 38.2 %collective-permute-start.37 = (bf16[2,256,512]{2,1,0:T(8,128)(2,1)S(1)}, bf16[2,256,512]{2,1,0:T(8,128)(2,1)S(1)}, u32[]{:S(2)}, u32[]{:S(2)}) collective-permute-start(bf16[2,256,512]{2,1,0:T(8,128)(2,1)S(1)} %get-tuple-element.63), channel_id=1, source_target_pairs={{0,16},{8,17},{2,18},{10,19},{4,20},{12,21},{6,22},{14,23},{1,24},... | collective-permute-start | bytes 1572872 | tf_op jit(solution)/shard_map/ppermute | solution.py:83
  194.2 38.2 %collective-permute-start.36 = (bf16[2,256,512]{2,1,0:T(8,128)(2,1)S(1)}, bf16[2,256,512]{2,1,0:T(8,128)(2,1)S(1)}, u32[]{:S(2)}, u32[]{:S(2)}) collective-permute-start(bf16[2,256,512]{2,1,0:T(8,128)(2,1)S(1)} %get-tuple-element.62), channel_id=1, source_target_pairs={{8,1},{10,3},{12,5},{14,7},{1,8},{3,10},{5,12},{7,14},{24,17},{26,... | collective-permute-start | bytes 1572872 | tf_op jit(solution)/shard_map/ppermute | solution.py:83
  196.4 45.1 %collective-permute-start.33 = (bf16[2,256,512]{2,1,0:T(8,128)(2,1)S(1)}, bf16[2,256,512]{2,1,0:T(8,128)(2,1)S(1)}, u32[]{:S(2)}, u32[]{:S(2)}) collective-permute-start(bf16[2,256,512]{2,1,0:T(8,128)(2,1)S(1)} %get-tuple-element.61), channel_id=1, source_target_pairs={{0,16},{8,17},{2,18},{10,19},{4,20},{12,21},{6,22},{14,23},{1,24},... | collective-permute-start | bytes 1572872 | tf_op jit(solution)/shard_map/ppermute | solution.py:83
  198.7 42.9 %collective-permute-start.32 = (bf16[2,256,512]{2,1,0:T(8,128)(2,1)S(1)}, bf16[2,256,512]{2,1,0:T(8,128)(2,1)S(1)}, u32[]{:S(2)}, u32[]{:S(2)}) collective-permute-start(bf16[2,256,512]{2,1,0:T(8,128)(2,1)S(1)} %get-tuple-element.60), channel_id=1, source_target_pairs={{8,1},{10,3},{12,5},{14,7},{1,8},{3,10},{5,12},{7,14},{24,17},{26,... | collective-permute-start | bytes 1572872 | tf_op jit(solution)/shard_map/ppermute | solution.py:83
  212.3 34.3 %collective-permute-start.26 = (bf16[128,1024]{0,1:T(8,128)(2,1)S(1)}, bf16[128,1024]{0,1:T(8,128)(2,1)S(1)}, u32[]{:S(2)}, u32[]{:S(2)}) collective-permute-start(bf16[128,1024]{0,1:T(8,128)(2,1)S(1)} %get-tuple-element.86), channel_id=1, source_target_pairs={{0,1},{1,0},{2,3},{3,2},{4,5},{5,4},{6,7},{7,6},{8,9},{9,8},{10,11... | collective-permute-start | bytes 786440 | tf_op jit(solution)/shard_map/ppermute | solution.py:83
  232.6 9.3 %copy-start.36 = (bf16[2,256,512]{2,1,0:T(8,128)(2,1)S(1)}, bf16[2,256,512]{2,1,0:T(8,128)(2,1)}, u32[]{:S(2)}) copy-start(bf16[2,256,512]{2,1,0:T(8,128)(2,1)} %param.13) | copy-start | bytes 1572868
  232.7 9.3 %copy-start.39 = (f32[2,256,512]{2,1,0:T(8,128)S(1)}, f32[2,256,512]{2,1,0:T(8,128)}, u32[]{:S(2)}) copy-start(f32[2,256,512]{2,1,0:T(8,128)} %param.15) | copy-start | bytes 3145732
  232.7 9.3 %copy-start.40 = (f32[2,256,512]{2,1,0:T(8,128)S(1)}, f32[2,256,512]{2,1,0:T(8,128)}, u32[]{:S(2)}) copy-start(f32[2,256,512]{2,1,0:T(8,128)} %param.16) | copy-start | bytes 3145732
  (19 other events, 44.0 us)
where the time goes:
time: 252 us; the launch traced here: 250 us
  waiting for transfers between devices  97.5 us (39%)
  starting transfers between devices  68.7 us (27%)
  matrix products  45.6 us (18%)
  other arithmetic  20.8 us (8%)
  local copies, waits for them, and re-layouts  14.5 us (6%)
  between operations  3.37 us (1%)
    ppermute x38, waiting for transfers between devices, send(): return lax.ppermute(value, AXES, [(a, b) for a, b in pairs if a != b])  97.5 us
    ppermute x38, starting transfers between devices, send(): return lax.ppermute(value, AXES, [(a, b) for a, b in pairs if a != b])  68.7 us
    dot_general x32, matrix products, dot_t(): lax.dot_general(a, b, (((1,), (1,)), ((), ())), preferred_element_type=jn...  26.1 us
    dot_general x8, matrix products, t_dot(): lax.dot_general(a, b, (((0,), (0,)), ((), ())), preferred_element_type=jn...  11.7 us
    dot_general x16, matrix products, dot(): return jnp.dot(a, b, preferred_element_type=jnp.float32)  7.82 us
    unnamed x109, local copies, waits for them, and re-layouts  7.41 us
  transfers between devices with their start and end apart: 38, of which 10 were waited for; matrix products, arithmetic and copies ran while one was open for 28% of the time, Pallas kernels for 0%

commit v1 on v0

--- a/solution.py
+++ b/solution.py
@@ -1,6 +1,7 @@
 import jax
 import jax.numpy as jnp
 from jax import lax
+from jax.experimental.layout import Layout, with_layout_constraint
 from jax.sharding import PartitionSpec as P
 
 STEP = 10
@@ -95,23 +96,29 @@
     return lax.dot_general(a, b, (((0,), (0,)), ((), ())), preferred_element_type=jnp.float32)
 
 
+def flipped(parts, label):
+    bit = 1
+    while bit < len(parts):
+        flip = (label & bit) != 0
+        parts = [jnp.where(flip, parts[n ^ bit], parts[n]) for n in range(len(parts))]
+        bit *= 2
+    return parts
+
+
 def placed_rows(pieces, label):
-    size = pieces[0].shape[0]
-    whole = jnp.zeros((size * len(pieces),) + pieces[0].shape[1:], pieces[0].dtype)
-    for m, piece in enumerate(pieces):
-        whole = lax.dynamic_update_slice_in_dim(whole, piece, (label ^ m) * size, 0)
-    return whole
+    return jnp.concatenate(flipped(pieces, label), axis=0)
 
 
 def placed_cols(pieces, label):
-    stacked = jnp.stack(pieces)
-    return jnp.concatenate(
-        [
-            lax.dynamic_index_in_dim(stacked, label ^ t, 0, keepdims=False)
-            for t in range(len(pieces))
-        ],
-        axis=1,
-    )
+    return jnp.concatenate(flipped(pieces, label), axis=1)
+
+
+def arrange(x, marks, label, spans, rows):
+    count = x.shape[1] // rows
+    parts = flipped([x[:, n * rows : (n + 1) * rows] for n in range(count)], label)
+    return [
+        jnp.concatenate([parts[o ^ at] for o in spans] + [marks], axis=1) for at in (0, 2)
+    ]
 
 
 CHUNKS = 2
@@ -138,9 +145,13 @@
     others = range(1, ctx // 2)
     bf16, f32 = jnp.bfloat16, jnp.float32
 
+    row_major = Layout(major_to_minor=(0, 1, 2))
     packed = [
-        jnp.concatenate(
-            [w[:, :, n * wide : (n + 1) * wide] for w in (filter_w, gate_w)], axis=2
+        with_layout_constraint(
+            jnp.concatenate(
+                [w[:, :, n * wide : (n + 1) * wide] for w in (filter_w, gate_w)], axis=2
+            ),
+            row_major,
         )
         for n in range(CHUNKS)
     ]
@@ -157,12 +168,6 @@
         block[n, j + 1] = send(block[n, j], inner(1, 0))
 
     mine = inputs[0]
-
-    def channels(label):
-        return jnp.concatenate(
-            [lax.dynamic_slice_in_dim(mine, (label ^ o) * rows, rows, 1) for o in spans] + [marks],
-            axis=1,
-        )
 
     def pair(own, got):
         low, high = jnp.where(core == 0, own, got), jnp.where(core == 0, got, own)
@@ -173,7 +178,8 @@
     fetch(0, 0)
     lanes = 128
     marks = jnp.broadcast_to((doc_ids[0] + 1).astype(bf16)[:, None], (tokens, lanes))
-    half = pair(channels(vi), send(channels(vi ^ 2), plain(0, 1)))
+    own_x, give_x = arrange(mine, marks, vi, spans, rows)
+    half = pair(own_x, send(give_x, plain(0, 1)))
 
     def odd(value):
         return jnp.concatenate(
@@ -226,23 +232,12 @@
         for q, x in enumerate(side)
     ]
 
-    own_cols = 2 * columns
-    cot_parts = [lax.dynamic_slice_in_dim(cotangent[0], vy * own_cols, own_cols, 1)] + [
-        send(
-            lax.dynamic_slice_in_dim(cotangent[0], (vy ^ dy) * own_cols, own_cols, 1),
-            plain(0, 2 * dy),
-        )
-        for dy in others
-    ]
-    cot_rows = jnp.stack(cot_parts)
-    cot_cuts = [
-        lax.dynamic_slice_in_dim(cot_rows, (core ^ e) * columns, columns, 2) for e in (0, 1)
-    ]
-    cot_got = [send(cot_cuts[e], enter(0, e)) for e in (0, 1)]
+    cot_cuts = flipped(
+        [cotangent[0][:, m * columns : (m + 1) * columns] for m in range(ctx)], c
+    )
+    cot_got = [send(cot_cuts[m], enter(0, m)) for m in range(ctx)]
     cot_got[0] = kept(cot_cuts[0], cot_got[0])
-    cot_cols = placed_rows(
-        [cot_got[m & 1][m >> 1] for m in range(ctx)], vc
-    )
+    cot_cols = placed_rows(cot_got, vc)
 
     gated, delta, grads, backs = [], [], [], []
     for n in range(CHUNKS):
@@ -286,7 +281,7 @@
         got[0] = kept(parts[:, 0], got[0])
         grads.append(got)
 
-    gated = jnp.concatenate(gated, axis=1)
+    gated = with_layout_constraint(jnp.concatenate(gated, axis=1), Layout(major_to_minor=(0, 1)))
     out_cuts = [
         lax.dynamic_slice_in_dim(gated, (vc ^ m) * tokens, tokens, 0) for m in range(ctx)
     ]
@@ -310,18 +305,21 @@
         chip_sums.append(kept_rows)
     chip_sum = in_order(*chip_sums)
     crossing = chip_sum[1].astype(bf16)
-    z_got = send(crossing, plain(2, 0)).astype(f32)
-    both_sum = (chip_sum[0] + z_got).astype(bf16)
-    keep = lax.dynamic_slice_in_dim(both_sum, core * tokens, tokens, 0)
-    give = lax.dynamic_slice_in_dim(both_sum, (1 - core) * tokens, tokens, 0)
-    got = send(give, plain(0, 1))
-    joined = jnp.concatenate([keep, got], axis=1)
-    where_is = []
-    for t in range(dp):
-        rel = vi ^ t
-        slot = (rel >> 2) * 2 + (rel & 1) + ((rel >> 1) & 1) * len(spans)
-        where_is.append(lax.dynamic_slice_in_dim(joined, slot * rows, rows, 1))
-    input_sum = jnp.concatenate(where_is, axis=1).astype(f32)
+    z_got = send(crossing, plain(2, 0))
+
+    def tokens_of(at):
+        return (
+            lax.dynamic_slice_in_dim(chip_sum[0], at * tokens, tokens, 0)
+            + lax.dynamic_slice_in_dim(z_got, at * tokens, tokens, 0).astype(f32)
+        ).astype(bf16)
+
+    got = send(tokens_of(1 - core), plain(0, 1))
+    keep = tokens_of(core)
+    parts = [None] * dp
+    for n, o in enumerate(spans):
+        cut = slice(n * rows, (n + 1) * rows)
+        parts[o], parts[o ^ 2] = keep[:, cut], got[:, cut]
+    input_sum = jnp.concatenate(flipped(parts, vi), axis=1).astype(f32)
     input_grad = (cotangent[0].astype(f32) + input_sum).astype(bf16)
 
     totals = []

time: 252 us -> 206 us (0.82)
  starting transfers between devices: 68.7 us -> 45.9 us
  matrix products: 45.6 us -> 25.2 us
  local copies, waits for them, and re-layouts: 14.5 us -> 3.86 us
  waiting for transfers between devices: 97.5 us -> 108 us
    ppermute x38 -> x39, starting transfers between devices: 68.7 us -> 45.9 us  [send(): return lax.ppermute(value, AXES, [(a, b) for a, b in pairs if a != b])]
    dot_general x32, matrix products: 26.1 us -> 11.9 us  [dot_t(): lax.dot_general(a, b, (((1,), (1,)), ((), ())), preferred_element_type=jn...]
    ppermute x38 -> x39, waiting for transfers between devices: 97.5 us -> 108 us  [send(): return lax.ppermute(value, AXES, [(a, b) for a, b in pairs if a != b])]
    unnamed x109 -> x21, local copies, waits for them, and re-layouts: 7.41 us -> 0.61 us
    dot_general x8, matrix products: 11.7 us -> 6.31 us  [t_dot(): lax.dot_general(a, b, (((0,), (0,)), ((), ())), preferred_element_type=jn...]
    unnamed x0 -> x13, other arithmetic: none -> 4.51 us
    dynamic_slice x21 -> x0, local copies, waits for them, and re-layouts: 3.9 us -> none  [the longest x9 2.07 us: channels(): lax.dynamic_slice_in_dim(mine, (label ^ o) * rows, rows, 1)]
  transfers between devices with their start and end apart: 38 -> 39, of which waited for: 10 -> 12; matrix products, arithmetic and copies ran while one was open for 28% -> 23% of each run, Pallas kernels for 0% -> 0%
where the time goes in v1:
time: 206 us
  waiting for transfers between devices  108 us (52%)
  starting transfers between devices  45.9 us (22%)
  matrix products  25.2 us (12%)
  other arithmetic  20.8 us (10%)
  local copies, waits for them, and re-layouts  3.86 us (2%)
  between operations  2.37 us (1%)
    ppermute x39, waiting for transfers between devices, send(): return lax.ppermute(value, AXES, [(a, b) for a, b in pairs if a != b])  108 us
    ppermute x39, starting transfers between devices, send(): return lax.ppermute(value, AXES, [(a, b) for a, b in pairs if a != b])  45.9 us
    dot_general x32, matrix products, dot_t(): lax.dot_general(a, b, (((1,), (1,)), ((), ())), preferred_element_type=jn...  11.9 us
    dot_general x16, matrix products, dot(): return jnp.dot(a, b, preferred_element_type=jnp.float32)  7.01 us
    dot_general x8, matrix products, t_dot(): lax.dot_general(a, b, (((0,), (0,)), ((), ())), preferred_element_type=jn...  6.31 us
    unnamed x13, other arithmetic  4.51 us
  transfers between devices with their start and end apart: 39, of which 12 were waited for; matrix products, arithmetic and copies ran while one was open for 23% of the time, Pallas kernels for 0%

profile of v1, /device:TPU:0, one launch (start us, length us, event | category | flops | bytes accessed | tf_op | source)
XLA Modules:
  0.0 206.0 jit_solution(8361949910022625498)
XLA Ops:
  0.7 1.3 fusion.126
  2.1 4.1 %collective-permute-start.6 = (bf16[2,256,512]{2,1,0:T(8,128)(2,1)S(1)}, bf16[2,256,512]{2,1,0:T(8,128)(2,1)S(1)}, u32[]{:S(2)}, u32[]{:S(2)}) collective-permute-start(bf16[2,256,512]{2,1,0:T(8,128)(2,1)S(1)} %pad_maximum_fusion.17), channel_id=1, source_target_pairs={{0,16},{1,24},{2,18},{3,26},{4,20},{5,28},{6,22},{7,30},{8,17},{9,... | collective-permute-start | bytes 1572872 | tf_op jit(solution)/shard_map/ppermute | solution.py:84
  6.2 0.8 broadcast_select_fusion.32
  7.0 1.0 collective-permute-start.18
  8.5 2.2 %collective-permute-start.20 = (bf16[128,512]{1,0:T(8,128)(2,1)}, bf16[128,512]{1,0:T(8,128)(2,1)}, u32[]{:S(2)}, u32[]{:S(2)}) collective-permute-start(bf16[128,512]{1,0:T(8,128)(2,1)} %get-tuple-element.101), channel_id=1, source_target_pairs={{0,8},{1,0},{2,10},{3,2},{4,12},{5,4},{6,14},{7,6},{8,9},{9,1},{10... | collective-permute-start | bytes 393224 | tf_op jit(solution)/shard_map/ppermute | solution.py:84
  10.7 1.3 collective-permute-start.21
  12.0 0.7 select_dynamic-update-slice_fusion.7
  12.7 0.7 select_dynamic-update-slice_fusion.6
  13.4 0.7 select_dynamic-update-slice_fusion.5
  14.1 0.7 select_dynamic-update-slice_fusion.4
  14.8 0.7 select_dynamic-update-slice_fusion.1
  15.5 0.7 select_dynamic-update-slice_fusion
  16.2 0.7 constant_dynamic-update-slice_fusion
  17.6 3.4 %collective-permute-done.18 = bf16[128,512]{1,0:T(8,128)(2,1)S(1)} collective-permute-done((bf16[128,512]{1,0:T(8,128)(2,1)}, bf16[128,512]{1,0:T(8,128)(2,1)S(1)}, u32[]{:S(2)}, u32[]{:S(2)}) %collective-permute-start.18) | collective-permute-done | bytes 131104 | tf_op jit(solution)/shard_map/ppermute | solution.py:84
  21.0 0.7 collective-permute-start.4
  21.7 4.7 %collective-permute-start = (bf16[128,1152]{1,0:T(8,128)(2,1)}, bf16[128,1152]{1,0:T(8,128)(2,1)S(1)}, u32[]{:S(2)}, u32[]{:S(2)}) collective-permute-start(bf16[128,1152]{1,0:T(8,128)(2,1)} %get-tuple-element.120), channel_id=1, source_target_pairs={{0,1},{1,0},{2,3},{3,2},{4,5},{5,4},{6,7},{7,6},{8,9},{9,8},{10,11... | collective-permute-start | bytes 884744 | tf_op jit(solution)/shard_map/ppermute | solution.py:84
  26.5 0.7 collective-permute-start.9
  27.2 1.0 broadcast_select_fusion.21
  28.2 1.2 broadcast_select_fusion.13
  29.5 3.0 %collective-permute-start.2 = (bf16[256,1152]{1,0:T(8,128)(2,1)S(1)}, bf16[256,1152]{1,0:T(8,128)(2,1)S(1)}, u32[]{:S(2)}, u32[]{:S(2)}) collective-permute-start(bf16[256,1152]{1,0:T(8,128)(2,1)S(1)} %pad_maximum_fusion.10), channel_id=1, source_target_pairs={{0,8},{1,9},{2,10},{3,11},{4,12},{5,13},{6,14},{7,15},{8,0},{9,1},... | collective-permute-start | bytes 1769480 | tf_op jit(solution)/shard_map/ppermute | solution.py:84
  33.1 1.6 collective-permute-start.28
  35.0 7.3 %collective-permute-done.28 = bf16[256,640]{1,0:T(8,128)(2,1)S(1)} collective-permute-done((bf16[256,640]{1,0:T(8,128)(2,1)S(1)}, bf16[256,640]{1,0:T(8,128)(2,1)S(1)}, u32[]{:S(2)}, u32[]{:S(2)}) %collective-permute-start.28) | collective-permute-done | bytes 327712 | tf_op jit(solution)/shard_map/ppermute | solution.py:84
  42.4 1.2 collective-permute-start.5
  43.6 20.5 %collective-permute-done.2 = bf16[256,1152]{1,0:T(8,128)(2,1)S(1)} collective-permute-done((bf16[256,1152]{1,0:T(8,128)(2,1)S(1)}, bf16[256,1152]{1,0:T(8,128)(2,1)S(1)}, u32[]{:S(2)}, u32[]{:S(2)}) %collective-permute-start.2) | collective-permute-done | bytes 589856 | tf_op jit(solution)/shard_map/ppermute | solution.py:84
  64.2 1.7 collective-permute-start.29
  65.9 1.0 collective-permute-start.3
  67.7 1.5 collective-permute-start.7
  69.2 5.6 %collective-permute-done.29 = bf16[256,640]{1,0:T(8,128)(2,1)S(1)} collective-permute-done((bf16[256,640]{1,0:T(8,128)(2,1)S(1)}, bf16[256,640]{1,0:T(8,128)(2,1)S(1)}, u32[]{:S(2)}, u32[]{:S(2)}) %collective-permute-start.29) | collective-permute-done | bytes 327712 | tf_op jit(solution)/shard_map/ppermute | solution.py:84
  74.8 1.6 collective-permute-start.12
  76.5 5.6 %collective-permute-done.3 = bf16[256,1152]{1,0:T(8,128)(2,1)S(1)} collective-permute-done((bf16[256,1152]{1,0:T(8,128)(2,1)S(1)}, bf16[256,1152]{1,0:T(8,128)(2,1)S(1)}, u32[]{:S(2)}, u32[]{:S(2)}) %collective-permute-start.3) | collective-permute-done | bytes 589856 | tf_op jit(solution)/shard_map/ppermute | solution.py:84
  82.1 1.0 collective-permute-start.30
  84.0 0.6 compare_reduce_fusion.3
  84.6 0.6 compare_reduce_fusion.2
  85.2 0.8 fusion.16
  87.6 9.1 %collective-permute-done.7 = bf16[2,256,512]{2,1,0:T(8,128)(2,1)S(1)} collective-permute-done((bf16[2,256,512]{2,1,0:T(8,128)(2,1)S(1)}, bf16[2,256,512]{2,1,0:T(8,128)(2,1)S(1)}, u32[]{:S(2)}, u32[]{:S(2)}) %collective-permute-start.7) | collective-permute-done | bytes 524320 | tf_op jit(solution)/shard_map/ppermute | solution.py:84
  100.4 1.9 collective-permute-done.12
  107.7 0.7 fusion.71
  108.5 0.9 fusion.72
  109.5 1.1 collective-permute-start.15
  110.7 0.7 collective-permute-start.17
  117.8 3.8 %collective-permute-start.24 = (bf16[512,512]{1,0:T(8,128)(2,1)S(1)}, bf16[512,512]{1,0:T(8,128)(2,1)S(1)}, u32[]{:S(2)}, u32[]{:S(2)}) collective-permute-start(bf16[512,512]{1,0:T(8,128)(2,1)S(1)} %pad_maximum_fusion.28), channel_id=1, source_target_pairs={{0,1},{8,9},{2,3},{10,11},{4,5},{12,13},{6,7},{14,15},{1,0},{9,8},... | collective-permute-start | bytes 1572872 | tf_op jit(solution)/shard_map/ppermute | solution.py:84
  121.5 1.5 collective-permute-start.35
  123.6 1.0 collective-permute-start.22
  124.7 0.9 add_convert_fusion.3
  132.0 1.0 collective-permute-start.25
  133.1 3.3 %collective-permute-done.35 = bf16[512,512]{1,0:T(8,128)(2,1)S(1)} collective-permute-done((bf16[512,512]{1,0:T(8,128)(2,1)S(1)}, bf16[512,512]{1,0:T(8,128)(2,1)S(1)}, u32[]{:S(2)}, u32[]{:S(2)}) %collective-permute-start.35) | collective-permute-done | bytes 524320 | tf_op jit(solution)/shard_map/ppermute | solution.py:84
  136.3 0.7 fusion.69
  137.1 0.7 fusion.18
  137.8 8.9 %collective-permute-done.31 = bf16[512,512]{1,0:T(8,128)(2,1)S(1)} collective-permute-done((bf16[512,512]{1,0:T(8,128)(2,1)S(1)}, bf16[512,512]{1,0:T(8,128)(2,1)S(1)}, u32[]{:S(2)}, u32[]{:S(2)}) %collective-permute-start.31) | collective-permute-done | bytes 524320 | tf_op jit(solution)/shard_map/ppermute | solution.py:84
  146.7 0.7 fusion.19
  147.4 1.0 fusion.70
  148.8 1.8 collective-permute-start.26
  150.7 0.7 add_convert_fusion
  151.5 2.1 %collective-permute-start.38 = (bf16[2,256,512]{2,1,0:T(8,128)(2,1)S(1)}, bf16[2,256,512]{2,1,0:T(8,128)(2,1)S(1)}, u32[]{:S(2)}, u32[]{:S(2)}) collective-permute-start(bf16[2,256,512]{2,1,0:T(8,128)(2,1)S(1)} %get-tuple-element.83), channel_id=1, source_target_pairs={{0,16},{8,17},{2,18},{10,19},{4,20},{12,21},{6,22},{14,23},{1,24},... | collective-permute-start | bytes 1572872 | tf_op jit(solution)/shard_map/ppermute | solution.py:84
  153.6 0.7 collective-permute-start.37
  154.3 0.7 add_convert_fusion.1
  155.1 1.0 collective-permute-start.34
  156.1 0.7 collective-permute-start.33
  156.8 13.3 %collective-permute-done.26 = bf16[256,1024]{1,0:T(8,128)(2,1)S(1)} collective-permute-done((bf16[256,1024]{1,0:T(8,128)(2,1)S(1)}, bf16[256,1024]{1,0:T(8,128)(2,1)S(1)}, u32[]{:S(2)}, u32[]{:S(2)}) %collective-permute-start.26) | collective-permute-done | bytes 524320 | tf_op jit(solution)/shard_map/ppermute | solution.py:84
  170.3 9.7 %collective-permute-done.38 = bf16[2,256,512]{2,1,0:T(8,128)(2,1)S(1)} collective-permute-done((bf16[2,256,512]{2,1,0:T(8,128)(2,1)S(1)}, bf16[2,256,512]{2,1,0:T(8,128)(2,1)S(1)}, u32[]{:S(2)}, u32[]{:S(2)}) %collective-permute-start.38) | collective-permute-done | bytes 524320 | tf_op jit(solution)/shard_map/ppermute | solution.py:84
  180.4 19.3 %collective-permute-done.34 = bf16[2,256,512]{2,1,0:T(8,128)(2,1)S(1)} collective-permute-done((bf16[2,256,512]{2,1,0:T(8,128)(2,1)S(1)}, bf16[2,256,512]{2,1,0:T(8,128)(2,1)S(1)}, u32[]{:S(2)}, u32[]{:S(2)}) %collective-permute-start.34) | collective-permute-done | bytes 524320 | tf_op jit(solution)/shard_map/ppermute | solution.py:84
  200.0 2.0 subtract_convert_fusion.1
  202.6 2.0 subtract_convert_fusion
  205.1 0.9 add_convert_fusion.2
  (173 shorter events, 29.6 us)
Async XLA Ops:
  0.6 5.6 %copy-start.1 = (bf16[1,128,2048]{2,1,0:T(8,128)(2,1)S(1)}, bf16[1,128,2048]{2,1,0:T(8,128)(2,1)}, u32[]{:S(2)}) copy-start(bf16[1,128,2048]{2,1,0:T(8,128)(2,1)} %param.19) | copy-start | bytes 1572868
  0.6 11.4 %copy-start = (bf16[1,128,2048]{2,1,0:T(8,128)(2,1)S(1)}, bf16[1,128,2048]{2,1,0:T(8,128)(2,1)}, u32[]{:S(2)}) copy-start(bf16[1,128,2048]{2,1,0:T(8,128)(2,1)} %param.10) | copy-start | bytes 1572868
  2.0 11.4 %copy-start.9 = (s32[1,128]{1,0:T(1,128)S(1)}, s32[1,128]{1,0:T(1,128)}, u32[]{:S(2)}) copy-start(s32[1,128]{1,0:T(1,128)} %param.11) | copy-start | bytes 1540
  2.1 65.1 %collective-permute-start.6 = (bf16[2,256,512]{2,1,0:T(8,128)(2,1)S(1)}, bf16[2,256,512]{2,1,0:T(8,128)(2,1)S(1)}, u32[]{:S(2)}, u32[]{:S(2)}) collective-permute-start(bf16[2,256,512]{2,1,0:T(8,128)(2,1)S(1)} %pad_maximum_fusion.17), channel_id=1, source_target_pairs={{0,16},{1,24},{2,18},{3,26},{4,20},{5,28},{6,22},{7,30},{8,17},{9,... | collective-permute-start | bytes 1572872 | tf_op jit(solution)/shard_map/ppermute | solution.py:84
  7.0 14.1 %collective-permute-start.18 = (bf16[128,512]{1,0:T(8,128)(2,1)}, bf16[128,512]{1,0:T(8,128)(2,1)S(1)}, u32[]{:S(2)}, u32[]{:S(2)}) collective-permute-start(bf16[128,512]{1,0:T(8,128)(2,1)} %get-tuple-element.99), channel_id=1, source_target_pairs={{0,10},{1,2},{2,8},{3,0},{4,14},{5,6},{6,12},{7,4},{8,11},{9,3},{1... | collective-permute-start | bytes 393224 | tf_op jit(solution)/shard_map/ppermute | solution.py:84
  7.9 13.8 %collective-permute-start.19 = (bf16[128,512]{1,0:T(8,128)(2,1)}, bf16[128,512]{1,0:T(8,128)(2,1)S(1)}, u32[]{:S(2)}, u32[]{:S(2)}) collective-permute-start(bf16[128,512]{1,0:T(8,128)(2,1)} %get-tuple-element.100), channel_id=1, source_target_pairs={{0,2},{1,10},{2,0},{3,8},{4,6},{5,14},{6,4},{7,12},{8,3},{9,11},{1... | collective-permute-start | bytes 393224 | tf_op jit(solution)/shard_map/ppermute | solution.py:84
  8.5 18.0 %collective-permute-start.20 = (bf16[128,512]{1,0:T(8,128)(2,1)}, bf16[128,512]{1,0:T(8,128)(2,1)}, u32[]{:S(2)}, u32[]{:S(2)}) collective-permute-start(bf16[128,512]{1,0:T(8,128)(2,1)} %get-tuple-element.101), channel_id=1, source_target_pairs={{0,8},{1,0},{2,10},{3,2},{4,12},{5,4},{6,14},{7,6},{8,9},{9,1},{10... | collective-permute-start | bytes 393224 | tf_op jit(solution)/shard_map/ppermute | solution.py:84
  10.7 16.5 %collective-permute-start.21 = (bf16[128,512]{1,0:T(8,128)(2,1)S(1)}, bf16[128,512]{1,0:T(8,128)(2,1)}, u32[]{:S(2)}, u32[]{:S(2)}) collective-permute-start(bf16[128,512]{1,0:T(8,128)(2,1)S(1)} %get-tuple-element.98), channel_id=1, source_target_pairs={{1,8},{3,10},{5,12},{7,14},{8,1},{10,3},{12,5},{14,7},{17,24},{19,... | collective-permute-start | bytes 393224 | tf_op jit(solution)/shard_map/ppermute | solution.py:84
  21.0 12.1 %collective-permute-start.4 = (bf16[2,256,512]{2,1,0:T(8,128)(2,1)S(1)}, bf16[2,256,512]{2,1,0:T(8,128)(2,1)S(1)}, u32[]{:S(2)}, u32[]{:S(2)}) collective-permute-start(bf16[2,256,512]{2,1,0:T(8,128)(2,1)S(1)} %pad_maximum_fusion.17), channel_id=1, source_target_pairs={{1,8},{3,10},{5,12},{7,14},{8,1},{10,3},{12,5},{14,7},{17,24},{19,... | collective-permute-start | bytes 1572872 | tf_op jit(solution)/shard_map/ppermute | solution.py:84
  21.7 6.5 %collective-permute-start = (bf16[128,1152]{1,0:T(8,128)(2,1)}, bf16[128,1152]{1,0:T(8,128)(2,1)S(1)}, u32[]{:S(2)}, u32[]{:S(2)}) collective-permute-start(bf16[128,1152]{1,0:T(8,128)(2,1)} %get-tuple-element.120), channel_id=1, source_target_pairs={{0,1},{1,0},{2,3},{3,2},{4,5},{5,4},{6,7},{7,6},{8,9},{9,8},{10,11... | collective-permute-start | bytes 884744 | tf_op jit(solution)/shard_map/ppermute | solution.py:84
  26.5 8.4 %collective-permute-start.9 = (bf16[2,256,512]{2,1,0:T(8,128)(2,1)S(1)}, bf16[2,256,512]{2,1,0:T(8,128)(2,1)S(1)}, u32[]{:S(2)}, u32[]{:S(2)}) collective-permute-start(bf16[2,256,512]{2,1,0:T(8,128)(2,1)S(1)} %pad_maximum_fusion.25), channel_id=1, source_target_pairs={{1,8},{3,10},{5,12},{7,14},{8,1},{10,3},{12,5},{14,7},{17,24},{19,... | collective-permute-start | bytes 1572872 | tf_op jit(solution)/shard_map/ppermute | solution.py:84
  28.2 77.7 %copy-start.4 = (bf16[512,512]{1,0:T(8,128)(2,1)}, bf16[512,512]{1,0:T(8,128)(2,1)S(1)}, u32[]{:S(2)}) copy-start(bf16[512,512]{1,0:T(8,128)(2,1)S(1)} %pad_maximum_fusion.26) | copy-start | bytes 1572868
  29.5 34.6 %collective-permute-start.2 = (bf16[256,1152]{1,0:T(8,128)(2,1)S(1)}, bf16[256,1152]{1,0:T(8,128)(2,1)S(1)}, u32[]{:S(2)}, u32[]{:S(2)}) collective-permute-start(bf16[256,1152]{1,0:T(8,128)(2,1)S(1)} %pad_maximum_fusion.10), channel_id=1, source_target_pairs={{0,8},{1,9},{2,10},{3,11},{4,12},{5,13},{6,14},{7,15},{8,0},{9,1},... | collective-permute-start | bytes 1769480 | tf_op jit(solution)/shard_map/ppermute | solution.py:84
  32.5 33.4 %collective-permute-start.1 = (bf16[256,1152]{1,0:T(8,128)(2,1)S(1)}, bf16[256,1152]{1,0:T(8,128)(2,1)S(1)}, u32[]{:S(2)}, u32[]{:S(2)}) collective-permute-start(bf16[256,1152]{1,0:T(8,128)(2,1)S(1)} %pad_maximum_fusion.10), channel_id=1, source_target_pairs={{0,2},{1,3},{2,0},{3,1},{4,6},{5,7},{6,4},{7,5},{8,10},{9,11},{10,... | collective-permute-start | bytes 1769480 | tf_op jit(solution)/shard_map/ppermute | solution.py:84
  33.1 9.2 %collective-permute-start.28 = (bf16[256,640]{1,0:T(8,128)(2,1)S(1)}, bf16[256,640]{1,0:T(8,128)(2,1)S(1)}, u32[]{:S(2)}, u32[]{:S(2)}) collective-permute-start(bf16[256,640]{1,0:T(8,128)(2,1)S(1)} %pad_maximum_fusion.45), channel_id=1, source_target_pairs={{0,4},{1,5},{2,6},{3,7},{4,0},{5,1},{6,2},{7,3},{8,12},{9,13},{10,... | collective-permute-start | bytes 983048 | tf_op jit(solution)/shard_map/ppermute | solution.py:84
  34.8 32.9 %collective-permute-start.11 = (bf16[2,256,512]{2,1,0:T(8,128)(2,1)S(1)}, bf16[2,256,512]{2,1,0:T(8,128)(2,1)S(1)}, u32[]{:S(2)}, u32[]{:S(2)}) collective-permute-start(bf16[2,256,512]{2,1,0:T(8,128)(2,1)S(1)} %pad_maximum_fusion.25), channel_id=1, source_target_pairs={{0,16},{1,24},{2,18},{3,26},{4,20},{5,28},{6,22},{7,30},{8,17},{9,... | collective-permute-start | bytes 1572872 | tf_op jit(solution)/shard_map/ppermute | solution.py:84
  42.4 44.3 %collective-permute-start.5 = (bf16[2,256,512]{2,1,0:T(8,128)(2,1)S(1)}, bf16[2,256,512]{2,1,0:T(8,128)(2,1)S(1)}, u32[]{:S(2)}, u32[]{:S(2)}) collective-permute-start(bf16[2,256,512]{2,1,0:T(8,128)(2,1)S(1)} %broadcast_select_fusion.11), channel_id=1, source_target_pairs={{0,4},{8,12},{2,6},{10,14},{4,0},{12,8},{6,2},{14,10},{1,5},{9,13}... | collective-permute-start | bytes 1572872 | tf_op jit(solution)/shard_map/ppermute | solution.py:84
  64.2 10.6 %collective-permute-start.29 = (bf16[256,640]{1,0:T(8,128)(2,1)S(1)}, bf16[256,640]{1,0:T(8,128)(2,1)S(1)}, u32[]{:S(2)}, u32[]{:S(2)}) collective-permute-start(bf16[256,640]{1,0:T(8,128)(2,1)S(1)} %pad_maximum_fusion.46), channel_id=1, source_target_pairs={{0,4},{1,5},{2,6},{3,7},{4,0},{5,1},{6,2},{7,3},{8,12},{9,13},{10,... | collective-permute-start | bytes 983048 | tf_op jit(solution)/shard_map/ppermute | solution.py:84
  65.9 16.2 %collective-permute-start.3 = (bf16[256,1152]{1,0:T(8,128)(2,1)S(1)}, bf16[256,1152]{1,0:T(8,128)(2,1)S(1)}, u32[]{:S(2)}, u32[]{:S(2)}) collective-permute-start(bf16[256,1152]{1,0:T(8,128)(2,1)S(1)} %collective-permute-done.2), channel_id=1, source_target_pairs={{0,2},{1,3},{2,0},{3,1},{4,6},{5,7},{6,4},{7,5},{8,10},{9,11},{10,... | collective-permute-start | bytes 1769480 | tf_op jit(solution)/shard_map/ppermute | solution.py:84
  67.1 31.5 %collective-permute-start.10 = (bf16[2,256,512]{2,1,0:T(8,128)(2,1)S(1)}, bf16[2,256,512]{2,1,0:T(8,128)(2,1)S(1)}, u32[]{:S(2)}, u32[]{:S(2)}) collective-permute-start(bf16[2,256,512]{2,1,0:T(8,128)(2,1)S(1)} %broadcast_select_fusion.10), channel_id=1, source_target_pairs={{0,4},{8,12},{2,6},{10,14},{4,0},{12,8},{6,2},{14,10},{1,5},{9,13}... | collective-permute-start | bytes 1572872 | tf_op jit(solution)/shard_map/ppermute | solution.py:84
  67.7 29.0 %collective-permute-start.7 = (bf16[2,256,512]{2,1,0:T(8,128)(2,1)S(1)}, bf16[2,256,512]{2,1,0:T(8,128)(2,1)S(1)}, u32[]{:S(2)}, u32[]{:S(2)}) collective-permute-start(bf16[2,256,512]{2,1,0:T(8,128)(2,1)S(1)} %collective-permute-done.6), channel_id=1, source_target_pairs={{0,4},{8,12},{2,6},{10,14},{4,0},{12,8},{6,2},{14,10},{1,5},{9,13}... | collective-permute-start | bytes 1572872 | tf_op jit(solution)/shard_map/ppermute | solution.py:84
  74.8 27.5 %collective-permute-start.12 = (bf16[2,256,512]{2,1,0:T(8,128)(2,1)S(1)}, bf16[2,256,512]{2,1,0:T(8,128)(2,1)S(1)}, u32[]{:S(2)}, u32[]{:S(2)}) collective-permute-start(bf16[2,256,512]{2,1,0:T(8,128)(2,1)S(1)} %collective-permute-done.11), channel_id=1, source_target_pairs={{0,4},{8,12},{2,6},{10,14},{4,0},{12,8},{6,2},{14,10},{1,5},{9,13}... | collective-permute-start | bytes 1572872 | tf_op jit(solution)/shard_map/ppermute | solution.py:84
  82.1 21.7 %collective-permute-start.30 = (bf16[256,1280]{1,0:T(8,128)(2,1)S(1)}, bf16[256,1280]{1,0:T(8,128)(2,1)S(1)}, u32[]{:S(2)}, u32[]{:S(2)}) collective-permute-start(bf16[256,1280]{1,0:T(8,128)(2,1)S(1)} %constant_dynamic-update-slice_fusion.2), channel_id=1, source_target_pairs={{0,2},{1,3},{2,0},{3,1},{4,6},{5,7},{6,4},{7,5},{8,10},{9,11},{10,... | collective-permute-start | bytes 1966088 | tf_op jit(solution)/shard_map/ppermute | solution.py:84
  97.1 8.3 %collective-permute-start.8 = (f32[512,512]{1,0:T(8,128)S(1)}, f32[512,512]{1,0:T(8,128)S(1)}, u32[]{:S(2)}, u32[]{:S(2)}) collective-permute-start(f32[512,512]{1,0:T(8,128)S(1)} %convolution_add_fusion.4), channel_id=1, source_target_pairs={{0,1},{8,9},{2,3},{10,11},{4,5},{12,13},{6,7},{14,15},{1,0},{9,8},... | collective-permute-start | bytes 3145736 | tf_op jit(solution)/shard_map/ppermute | solution.py:84
  102.8 4.1 %collective-permute-start.13 = (f32[512,512]{1,0:T(8,128)S(1)}, f32[512,512]{1,0:T(8,128)S(1)}, u32[]{:S(2)}, u32[]{:S(2)}) collective-permute-start(f32[512,512]{1,0:T(8,128)S(1)} %convolution_add_fusion), channel_id=1, source_target_pairs={{0,1},{8,9},{2,3},{10,11},{4,5},{12,13},{6,7},{14,15},{1,0},{9,8},... | collective-permute-start | bytes 3145736 | tf_op jit(solution)/shard_map/ppermute | solution.py:84
  106.3 1.0 slice-start
  106.3 19.3 %collective-permute-start.23 = (bf16[512,512]{1,0:T(8,128)(2,1)S(1)}, bf16[512,512]{1,0:T(8,128)(2,1)S(1)}, u32[]{:S(2)}, u32[]{:S(2)}) collective-permute-start(bf16[512,512]{1,0:T(8,128)(2,1)S(1)} %pad_maximum_fusion.27), channel_id=1, source_target_pairs={{0,1},{8,9},{2,3},{10,11},{4,5},{12,13},{6,7},{14,15},{1,0},{9,8},... | collective-permute-start | bytes 1572872 | tf_op jit(solution)/shard_map/ppermute | solution.py:84
  109.5 8.3 %collective-permute-start.15 = (bf16[128,512]{1,0:T(8,128)(2,1)S(1)}, bf16[128,512]{1,0:T(8,128)(2,1)S(1)}, u32[]{:S(2)}, u32[]{:S(2)}) collective-permute-start(bf16[128,512]{1,0:T(8,128)(2,1)S(1)} %get-tuple-element.107), channel_id=1, source_target_pairs={{0,2},{8,3},{2,0},{10,1},{4,6},{12,7},{6,4},{14,5},{1,10},{9,11},{... | collective-permute-start | bytes 393224 | tf_op jit(solution)/shard_map/ppermute | solution.py:84
  110.6 10.9 %collective-permute-start.14 = (bf16[128,512]{1,0:T(8,128)(2,1)S(1)}, bf16[128,512]{1,0:T(8,128)(2,1)S(1)}, u32[]{:S(2)}, u32[]{:S(2)}) collective-permute-start(bf16[128,512]{1,0:T(8,128)(2,1)S(1)} %get-tuple-element.106), channel_id=1, source_target_pairs={{0,3},{8,2},{2,1},{10,0},{4,7},{12,6},{6,5},{14,4},{1,11},{9,10},{... | collective-permute-start | bytes 393224 | tf_op jit(solution)/shard_map/ppermute | solution.py:84
  110.7 12.3 %collective-permute-start.16 = (bf16[128,512]{1,0:T(8,128)(2,1)S(1)}, bf16[128,512]{1,0:T(8,128)(2,1)S(1)}, u32[]{:S(2)}, u32[]{:S(2)}) collective-permute-start(bf16[128,512]{1,0:T(8,128)(2,1)S(1)} %get-tuple-element.108), channel_id=1, source_target_pairs={{0,1},{8,0},{2,3},{10,2},{4,5},{12,4},{6,7},{14,6},{1,9},{9,8},{3,... | collective-permute-start | bytes 393224 | tf_op jit(solution)/shard_map/ppermute | solution.py:84
  110.7 12.9 %collective-permute-start.17 = (bf16[128,512]{1,0:T(8,128)(2,1)S(1)}, bf16[128,512]{1,0:T(8,128)(2,1)S(1)}, u32[]{:S(2)}, u32[]{:S(2)}) collective-permute-start(bf16[128,512]{1,0:T(8,128)(2,1)S(1)} %get-tuple-element.105), channel_id=1, source_target_pairs={{8,1},{10,3},{12,5},{14,7},{1,8},{3,10},{5,12},{7,14},{24,17},{26,... | collective-permute-start | bytes 393224 | tf_op jit(solution)/shard_map/ppermute | solution.py:84
  117.8 8.6 %collective-permute-start.24 = (bf16[512,512]{1,0:T(8,128)(2,1)S(1)}, bf16[512,512]{1,0:T(8,128)(2,1)S(1)}, u32[]{:S(2)}, u32[]{:S(2)}) collective-permute-start(bf16[512,512]{1,0:T(8,128)(2,1)S(1)} %pad_maximum_fusion.28), channel_id=1, source_target_pairs={{0,1},{8,9},{2,3},{10,11},{4,5},{12,13},{6,7},{14,15},{1,0},{9,8},... | collective-permute-start | bytes 1572872 | tf_op jit(solution)/shard_map/ppermute | solution.py:84
  121.5 14.8 %collective-permute-start.35 = (bf16[512,512]{1,0:T(8,128)(2,1)S(1)}, bf16[512,512]{1,0:T(8,128)(2,1)S(1)}, u32[]{:S(2)}, u32[]{:S(2)}) collective-permute-start(bf16[512,512]{1,0:T(8,128)(2,1)S(1)} %pad_maximum_fusion.28), channel_id=1, source_target_pairs={{0,4},{8,12},{2,6},{10,14},{4,0},{12,8},{6,2},{14,10},{1,5},{9,13}... | collective-permute-start | bytes 1572872 | tf_op jit(solution)/shard_map/ppermute | solution.py:84
  123.0 23.7 %collective-permute-start.31 = (bf16[512,512]{1,0:T(8,128)(2,1)S(1)}, bf16[512,512]{1,0:T(8,128)(2,1)S(1)}, u32[]{:S(2)}, u32[]{:S(2)}) collective-permute-start(bf16[512,512]{1,0:T(8,128)(2,1)S(1)} %pad_maximum_fusion.27), channel_id=1, source_target_pairs={{0,4},{8,12},{2,6},{10,14},{4,0},{12,8},{6,2},{14,10},{1,5},{9,13}... | collective-permute-start | bytes 1572872 | tf_op jit(solution)/shard_map/ppermute | solution.py:84
  123.6 24.8 %collective-permute-start.22 = (bf16[256,1024]{1,0:T(8,128)(2,1)S(1)}, bf16[256,1024]{1,0:T(8,128)(2,1)S(1)}, u32[]{:S(2)}, u32[]{:S(2)}) collective-permute-start(bf16[256,1024]{1,0:T(8,128)(2,1)S(1)} %dynamic-slice_convert_fusion.1), channel_id=1, source_target_pairs={{0,2},{1,3},{2,0},{3,1},{4,6},{5,7},{6,4},{7,5},{8,10},{9,11},{10,... | collective-permute-start | bytes 1572872 | tf_op jit(solution)/shard_map/ppermute | solution.py:84
  132.0 16.4 %collective-permute-start.25 = (bf16[256,1024]{1,0:T(8,128)(2,1)S(1)}, bf16[256,1024]{1,0:T(8,128)(2,1)S(1)}, u32[]{:S(2)}, u32[]{:S(2)}) collective-permute-start(bf16[256,1024]{1,0:T(8,128)(2,1)S(1)} %dynamic-slice_convert_fusion), channel_id=1, source_target_pairs={{0,2},{1,3},{2,0},{3,1},{4,6},{5,7},{6,4},{7,5},{8,10},{9,11},{10,... | collective-permute-start | bytes 1572872 | tf_op jit(solution)/shard_map/ppermute | solution.py:84
  136.3 14.3 %collective-permute-start.36 = (bf16[512,512]{1,0:T(8,128)(2,1)S(1)}, bf16[512,512]{1,0:T(8,128)(2,1)S(1)}, u32[]{:S(2)}, u32[]{:S(2)}) collective-permute-start(bf16[512,512]{1,0:T(8,128)(2,1)S(1)} %collective-permute-done.35), channel_id=1, source_target_pairs={{0,1},{8,9},{2,3},{10,11},{4,5},{12,13},{6,7},{14,15},{1,0},{9,8},... | collective-permute-start | bytes 1572872 | tf_op jit(solution)/shard_map/ppermute | solution.py:84
  146.7 7.6 %collective-permute-start.32 = (bf16[512,512]{1,0:T(8,128)(2,1)S(1)}, bf16[512,512]{1,0:T(8,128)(2,1)S(1)}, u32[]{:S(2)}, u32[]{:S(2)}) collective-permute-start(bf16[512,512]{1,0:T(8,128)(2,1)S(1)} %collective-permute-done.31), channel_id=1, source_target_pairs={{0,1},{8,9},{2,3},{10,11},{4,5},{12,13},{6,7},{14,15},{1,0},{9,8},... | collective-permute-start | bytes 1572872 | tf_op jit(solution)/shard_map/ppermute | solution.py:84
  148.8 21.2 %collective-permute-start.26 = (bf16[256,1024]{1,0:T(8,128)(2,1)S(1)}, bf16[256,1024]{1,0:T(8,128)(2,1)S(1)}, u32[]{:S(2)}, u32[]{:S(2)}) collective-permute-start(bf16[256,1024]{1,0:T(8,128)(2,1)S(1)} %get-tuple-element.50), channel_id=1, source_target_pairs={{0,8},{1,9},{2,10},{3,11},{4,12},{5,13},{6,14},{7,15},{8,0},{9,1},... | collective-permute-start | bytes 1572872 | tf_op jit(solution)/shard_map/ppermute | solution.py:84
  151.5 28.5 %collective-permute-start.38 = (bf16[2,256,512]{2,1,0:T(8,128)(2,1)S(1)}, bf16[2,256,512]{2,1,0:T(8,128)(2,1)S(1)}, u32[]{:S(2)}, u32[]{:S(2)}) collective-permute-start(bf16[2,256,512]{2,1,0:T(8,128)(2,1)S(1)} %get-tuple-element.83), channel_id=1, source_target_pairs={{0,16},{8,17},{2,18},{10,19},{4,20},{12,21},{6,22},{14,23},{1,24},... | collective-permute-start | bytes 1572872 | tf_op jit(solution)/shard_map/ppermute | solution.py:84
  153.6 26.4 %collective-permute-start.37 = (bf16[2,256,512]{2,1,0:T(8,128)(2,1)S(1)}, bf16[2,256,512]{2,1,0:T(8,128)(2,1)S(1)}, u32[]{:S(2)}, u32[]{:S(2)}) collective-permute-start(bf16[2,256,512]{2,1,0:T(8,128)(2,1)S(1)} %get-tuple-element.82), channel_id=1, source_target_pairs={{8,1},{10,3},{12,5},{14,7},{1,8},{3,10},{5,12},{7,14},{24,17},{26,... | collective-permute-start | bytes 1572872 | tf_op jit(solution)/shard_map/ppermute | solution.py:84
  155.1 44.5 %collective-permute-start.34 = (bf16[2,256,512]{2,1,0:T(8,128)(2,1)S(1)}, bf16[2,256,512]{2,1,0:T(8,128)(2,1)S(1)}, u32[]{:S(2)}, u32[]{:S(2)}) collective-permute-start(bf16[2,256,512]{2,1,0:T(8,128)(2,1)S(1)} %get-tuple-element.81), channel_id=1, source_target_pairs={{0,16},{8,17},{2,18},{10,19},{4,20},{12,21},{6,22},{14,23},{1,24},... | collective-permute-start | bytes 1572872 | tf_op jit(solution)/shard_map/ppermute | solution.py:84
  156.1 43.5 %collective-permute-start.33 = (bf16[2,256,512]{2,1,0:T(8,128)(2,1)S(1)}, bf16[2,256,512]{2,1,0:T(8,128)(2,1)S(1)}, u32[]{:S(2)}, u32[]{:S(2)}) collective-permute-start(bf16[2,256,512]{2,1,0:T(8,128)(2,1)S(1)} %get-tuple-element.80), channel_id=1, source_target_pairs={{8,1},{10,3},{12,5},{14,7},{1,8},{3,10},{5,12},{7,14},{24,17},{26,... | collective-permute-start | bytes 1572872 | tf_op jit(solution)/shard_map/ppermute | solution.py:84
  170.2 34.4 %collective-permute-start.27 = (bf16[128,1024]{1,0:T(8,128)(2,1)S(1)}, bf16[128,1024]{1,0:T(8,128)(2,1)S(1)}, u32[]{:S(2)}, u32[]{:S(2)}) collective-permute-start(bf16[128,1024]{1,0:T(8,128)(2,1)S(1)} %get-tuple-element.54), channel_id=1, source_target_pairs={{0,1},{1,0},{2,3},{3,2},{4,5},{5,4},{6,7},{7,6},{8,9},{9,8},{10,11... | collective-permute-start | bytes 786440 | tf_op jit(solution)/shard_map/ppermute | solution.py:84
  180.3 19.6 %copy-start.2 = (bf16[2,256,512]{2,1,0:T(8,128)(2,1)S(1)}, bf16[2,256,512]{2,1,0:T(8,128)(2,1)}, u32[]{:S(2)}) copy-start(bf16[2,256,512]{2,1,0:T(8,128)(2,1)} %param.13) | copy-start | bytes 1572868
  180.3 19.6 %copy-start.5 = (f32[2,256,512]{2,1,0:T(8,128)S(1)}, f32[2,256,512]{2,1,0:T(8,128)}, u32[]{:S(2)}) copy-start(f32[2,256,512]{2,1,0:T(8,128)} %param.15) | copy-start | bytes 3145732
  180.3 19.6 %copy-start.6 = (f32[2,256,512]{2,1,0:T(8,128)S(1)}, f32[2,256,512]{2,1,0:T(8,128)}, u32[]{:S(2)}) copy-start(f32[2,256,512]{2,1,0:T(8,128)} %param.16) | copy-start | bytes 3145732
  200.0 2.1 %copy-start.3 = (bf16[2,256,512]{2,1,0:T(8,128)(2,1)S(1)}, bf16[2,256,512]{2,1,0:T(8,128)(2,1)}, u32[]{:S(2)}) copy-start(bf16[2,256,512]{2,1,0:T(8,128)(2,1)} %param.14) | copy-start | bytes 1572868
  200.0 2.1 %copy-start.7 = (f32[2,256,512]{2,1,0:T(8,128)S(1)}, f32[2,256,512]{2,1,0:T(8,128)}, u32[]{:S(2)}) copy-start(f32[2,256,512]{2,1,0:T(8,128)} %param.17) | copy-start | bytes 3145732
  200.0 2.6 %copy-start.8 = (f32[2,256,512]{2,1,0:T(8,128)S(1)}, f32[2,256,512]{2,1,0:T(8,128)}, u32[]{:S(2)}) copy-start(f32[2,256,512]{2,1,0:T(8,128)} %param.18) | copy-start | bytes 3145732
